TPU v7x, 32 devices: a whole 2x2x4 slice. The times are simulated.
32 devices in a mesh: groups: 2 (over x), grid: 8 (over z, y), dp: 2 (over core).
Axes of the slice: x: 2, y: 2, z: 4, core: 2. Of those that a mesh axis runs over, the one named last changes fastest.
Arguments:
- acts: bfloat16 [4, 8, 192, 2560], P(('groups', 'dp'), 'grid'), parts along dimension 0, may hold values from -6 to 6
- cotangent: bfloat16 [4, 8, 192, 2560], P(('groups', 'dp'), 'grid'), parts along dimension 0, may hold values from -1.5 to 1.5
- w_gate: bfloat16 [8, 2560, 1792], P('grid'), may hold values from -0.078125 to 0.078125
- w_up: bfloat16 [8, 2560, 1792], P('grid'), may hold values from -0.078125 to 0.078125
- w_down: bfloat16 [8, 1792, 2560], P('grid'), may hold values from -0.0625 to 0.0625
Outputs:
- block_out: bfloat16 [4, 8, 192, 2560], P(('groups', 'dp'), 'grid'), parts along dimension 0
- input_grad: bfloat16 [4, 8, 192, 2560], P(('groups', 'dp'), 'grid'), parts along dimension 0
- gate_grad: bfloat16 [16, 2560, 1792], P(('groups', 'grid')), parts along dimension 0
- up_grad: bfloat16 [16, 2560, 1792], P(('groups', 'grid')), parts along dimension 0
- down_grad: bfloat16 [16, 1792, 2560], P(('groups', 'grid')), parts along dimension 0
There are 2 independent parts, one for each index of `groups`. A program takes and returns all parts, laid end to end along the dimension named above; an argument that names none is the same for every part. Nothing has to cross between parts.
All inputs are finite; a program needn't handle non-finite values.
Results may differ from a plain program's by a relative error of at most 0.015.
Values may be sent and summed in bfloat16 or wider, within the bound.
A program may use at most 192 MiB of HBM per device.

v0:
```python
import jax
import jax.numpy as jnp
from jax import lax
from jax.sharding import PartitionSpec as P


def from_partner(block, axis, stride):
    count = lax.axis_size(axis)
    route = []
    for low in range(count):
        high = low | 1 << stride
        if high != low and high < count:
            route += [(low, high), (high, low)]
    return lax.ppermute(block, axis, route)


def contract_rows(left, right):
    return lax.dot_general(
        left, right, (((0,), (0,)), ((), ())), preferred_element_type=jnp.float32
    )


def contract_cols(left, right):
    return lax.dot_general(
        left, right, (((1,), (1,)), ((), ())), preferred_element_type=jnp.float32
    )


def order_pair(is_upper, mine, other):
    return jnp.where(is_upper, jnp.concatenate([other, mine], 1), jnp.concatenate([mine, other], 1))


def column_sum(partial_term, total_rows, col_bits, row_bits, my_row):
    result_sum = partial_term(0, total_rows)
    for level_bit in range(row_bits - 1, -1, -1):
        half_rows = result_sum.shape[1] // 2
        lower_half = result_sum[:, :half_rows]
        upper_half = result_sum[:, half_rows:]
        is_upper = my_row >> level_bit & 1 == 1
        kept_half = jnp.where(is_upper, upper_half, lower_half)
        given_half = jnp.where(is_upper, lower_half, upper_half)
        result_sum = kept_half + from_partner(
            given_half.astype(jnp.bfloat16), "grid", col_bits + level_bit
        ).astype(given_half.dtype)
    return result_sum


def column_gather(pieces, col_bits, row_bits, my_row):
    for level_bit in range(row_bits):
        partner = from_partner(pieces, "grid", col_bits + level_bit)
        pieces = order_pair(my_row >> level_bit & 1 == 1, pieces, partner)
    return pieces


def row_sum(full_sum, col_bits, my_col):
    for level_bit in range(col_bits - 1, -1, -1):
        half_rows = full_sum.shape[0] // 2
        lower_half = full_sum[:half_rows]
        upper_half = full_sum[half_rows:]
        is_upper = my_col >> level_bit & 1 == 1
        kept_half = jnp.where(is_upper, upper_half, lower_half)
        given_half = jnp.where(is_upper, lower_half, upper_half)
        full_sum = kept_half + from_partner(
            given_half.astype(jnp.bfloat16), "grid", level_bit
        ).astype(given_half.dtype)
    return full_sum


def per_device(acts, cotangent, w_gate, w_up, w_down):
    grid_size = lax.axis_size("grid")
    grid_cols = min(8, grid_size // 2)
    grid_rows = grid_size // grid_cols
    col_bits = grid_cols.bit_length() - 1
    row_bits = grid_rows.bit_length() - 1
    position = lax.axis_index("grid")
    my_row = position // grid_cols
    my_col = position % grid_cols
    own_acts = acts[0, 0]
    own_grads = cotangent[0, 0]
    gate_tile = w_gate[0]
    up_tile = w_up[0]
    down_tile = w_down[0]
    gathered = jnp.stack([own_acts, own_grads])
    for level_bit in range(col_bits):
        partner = from_partner(gathered, "grid", level_bit)
        gathered = order_pair(my_col >> level_bit & 1 == 1, gathered, partner)
    inputs_row = gathered[0]
    out_grad_row = gathered[1]
    total_rows = inputs_row.shape[0]

    def gate_up_term(row_start, row_count):
        return jnp.stack(
            [
                jnp.dot(inputs_row, gate_tile, preferred_element_type=jnp.float32),
                jnp.dot(inputs_row, up_tile, preferred_element_type=jnp.float32),
            ]
        )

    summed = column_sum(gate_up_term, total_rows, col_bits, row_bits, my_row)
    gate_pre = summed[0]
    up_proj = summed[1]
    sigmoid_g = jax.nn.sigmoid(gate_pre)
    activated = gate_pre * sigmoid_g
    hidden = (activated * up_proj).astype(jnp.bfloat16)
    hidden_full = column_gather(hidden[None], col_bits, row_bits, my_row)[0]
    output_sum = row_sum(
        jnp.dot(hidden_full, down_tile, preferred_element_type=jnp.float32), col_bits, my_col
    )
    block_out = (own_acts.astype(jnp.float32) + output_sum).astype(jnp.bfloat16)

    def hidden_grad_term(row_start, row_count):
        return contract_cols(out_grad_row, down_tile)[None]

    hidden_grad = column_sum(hidden_grad_term, total_rows, col_bits, row_bits, my_row)[0]
    gate_back = (hidden_grad * up_proj * sigmoid_g * (1.0 + gate_pre * (1.0 - sigmoid_g))).astype(
        jnp.bfloat16
    )
    up_back = (hidden_grad * activated).astype(jnp.bfloat16)
    backs_full = column_gather(jnp.stack([gate_back, up_back]), col_bits, row_bits, my_row)
    down_local = contract_rows(hidden_full, out_grad_row)
    input_part = contract_cols(backs_full[0], gate_tile) + contract_cols(backs_full[1], up_tile)
    input_sum = row_sum(input_part, col_bits, my_col)
    input_grad = (own_grads.astype(jnp.float32) + input_sum).astype(jnp.bfloat16)
    gate_local = contract_rows(inputs_row, backs_full[0])
    up_local = contract_rows(inputs_row, backs_full[1])
    gate_total, up_total, down_total = (
        lax.psum(gate_local.astype(jnp.bfloat16), "dp").astype(jnp.float32),
        lax.psum(up_local.astype(jnp.bfloat16), "dp").astype(jnp.float32),
        lax.psum(down_local.astype(jnp.bfloat16), "dp").astype(jnp.float32),
    )
    return (
        block_out[None, None],
        input_grad[None, None],
        gate_total.astype(jnp.bfloat16)[None],
        up_total.astype(jnp.bfloat16)[None],
        down_total.astype(jnp.bfloat16)[None],
    )


def solution(mesh):
    return jax.shard_map(
        per_device,
        mesh=mesh,
        in_specs=(
            P(("groups", "dp"), "grid", None, None),
            P(("groups", "dp"), "grid", None, None),
            P("grid", None, None),
            P("grid", None, None),
            P("grid", None, None),
        ),
        out_specs=(
            P(("groups", "dp"), "grid", None, None),
            P(("groups", "dp"), "grid", None, None),
            P(("groups", "grid"), None, None),
            P(("groups", "grid"), None, None),
            P(("groups", "grid"), None, None),
        ),
        check_vma=False,
    )
```

profile of v0, /device:TPU:0, one launch (start us, length us, event | category | flops | bytes accessed | tf_op | source)
XLA Modules:
  0.0 722.5 jit_solution(10330217533321276245)
XLA Ops:
  7.2 3.1 pad_maximum_fusion.2
  10.3 3.0 collective-permute-start
  13.3 43.1 %collective-permute-done = bf16[2,192,2560]{2,1,0:T(8,128)(2,1)} collective-permute-done((bf16[2,192,2560]{2,1,0:T(8,128)(2,1)}, bf16[2,192,2560]{2,1,0:T(8,128)(2,1)}, u32[]{:S(2)}, u32[]{:S(2)}) %collective-permute-start) | collective-permute-done | bytes 1966112 | tf_op jit(solution)/shard_map/ppermute | solution.py:14
  56.5 4.0 maximum_select_fusion.2
  62.2 84.6 %collective-permute-done.1 = bf16[2,384,2560]{2,1,0:T(8,128)(2,1)} collective-permute-done((bf16[2,384,2560]{2,1,0:T(8,128)(2,1)}, bf16[2,384,2560]{2,1,0:T(8,128)(2,1)}, u32[]{:S(2)}, u32[]{:S(2)}) %collective-permute-start.1) | collective-permute-done | bytes 3932192 | tf_op jit(solution)/shard_map/ppermute | solution.py:14
  146.9 6.7 maximum_select_fusion
  153.6 13.7 %fusion.22 = f32[1,768,1792]{2,1,0:T(8,128)S(1)} fusion(bf16[1,2560,1792]{2,1,0:T(8,128)(2,1)} %param.8, bf16[2,768,2560]{2,1,0:T(8,128)(2,1)S(1)} %maximum_select_fusion), kind=kOutput, calls=%fused_computation.35 | convolution fusion | flops 7046430720 | bytes 18612224 | tf_op jit(solution)/shard_map/dot_general | solution.py:95
  167.3 10.9 %fusion.19 = f32[1,768,1792]{2,1,0:T(8,128)S(1)} fusion(bf16[1,2560,1792]{2,1,0:T(8,128)(2,1)} %param.7, bf16[2,768,2560]{2,1,0:T(8,128)(2,1)S(1)} %maximum_select_fusion), kind=kOutput, calls=%fused_computation.34 | convolution fusion | flops 7046430720 | bytes 18612224 | tf_op jit(solution)/shard_map/dot_general | solution.py:94
  178.2 2.0 select_convert_fusion
  180.1 2.5 collective-permute-start.2
  182.7 10.6 %fusion.25 = f32[1,768,1792]{2,1,0:T(8,128)S(1)} fusion(bf16[1,1792,2560]{2,1,0:T(8,128)(2,1)} %param.9, bf16[2,768,2560]{2,1,0:T(8,128)(2,1)} %copy-done.4), kind=kOutput, calls=%fused_computation.36 | convolution fusion | flops 7046430720 | bytes 18612224 | tf_op jit(solution)/shard_map/dot_general | solution.py:24
  194.0 136.6 %collective-permute-done.2 = bf16[2,384,1792]{2,1,0:T(8,128)(2,1)} collective-permute-done((bf16[2,384,1792]{2,1,0:T(8,128)(2,1)}, bf16[2,384,1792]{2,1,0:T(8,128)(2,1)}, u32[]{:S(2)}, u32[]{:S(2)}) %collective-permute-start.2) | collective-permute-done | bytes 2752544 | tf_op jit(solution)/shard_map/ppermute | solution.py:14
  330.6 2.5 convert_add_fusion
  333.1 26.1 %collective-permute-done.6 = bf16[1,384,1792]{2,1,0:T(8,128)(2,1)S(1)} collective-permute-done((bf16[1,384,1792]{2,1,0:T(8,128)(2,1)S(1)}, bf16[1,384,1792]{2,1,0:T(8,128)(2,1)S(1)}, u32[]{:S(2)}, u32[]{:S(2)}) %collective-permute-start.6) | collective-permute-done | bytes 1376288 | tf_op jit(solution)/shard_map/ppermute | solution.py:14
  359.2 1.9 multiply_convert_fusion.1
  361.4 3.0 collective-permute-start.7
  364.4 118.8 %collective-permute-done.3 = bf16[1,384,1792]{2,1,0:T(8,128)(2,1)S(1)} collective-permute-done((bf16[1,384,1792]{2,1,0:T(8,128)(2,1)S(1)}, bf16[1,384,1792]{2,1,0:T(8,128)(2,1)S(1)}, u32[]{:S(2)}, u32[]{:S(2)}) %collective-permute-start.3) | collective-permute-done | bytes 1376288 | tf_op jit(solution)/shard_map/ppermute | solution.py:14
  483.2 12.8 %fusion.2 = bf16[1,1792,2560]{2,1,0:T(8,128)(2,1)} fusion(bf16[2,768,2560]{2,1,0:T(8,128)(2,1)} %copy-done.4, bf16[384,1792]{1,0:T(8,128)(2,1)} %bitcast.73, bf16[384,1792]{1,0:T(8,128)(2,1)S(1)} %bitcast.75, pred[]{:T(512)S(6)} %eq.10), kind=kOutput, calls=%fused_computation.7 | convolution fusion | flops 7063404544 | bytes 15859713 | tf_op jit(solution)/shard_map/dot_general | solution.py:18
  496.1 44.9 %collective-permute-done.7 = bf16[2,384,1792]{2,1,0:T(8,128)(2,1)S(1)} collective-permute-done((bf16[2,384,1792]{2,1,0:T(8,128)(2,1)S(1)}, bf16[2,384,1792]{2,1,0:T(8,128)(2,1)S(1)}, u32[]{:S(2)}, u32[]{:S(2)}) %collective-permute-start.7) | collective-permute-done | bytes 2752544 | tf_op jit(solution)/shard_map/ppermute | solution.py:14
  540.9 5.3 maximum_select_fusion.1
  546.3 10.0 %fusion.1 = bf16[1,2560,1792]{2,1,0:T(8,128)(2,1)} fusion(bf16[2,768,2560]{2,1,0:T(8,128)(2,1)S(1)} %bitcast.72, bf16[2,768,1792]{2,1,0:T(8,128)(2,1)S(1)} %maximum_select_fusion.1), kind=kOutput, calls=%fused_computation.6 | convolution fusion | flops 7051018240 | bytes 15859712 | tf_op jit(solution)/shard_map/dot_general | solution.py:18
  556.3 9.8 %fusion = bf16[1,2560,1792]{2,1,0:T(8,128)(2,1)} fusion(bf16[2,768,2560]{2,1,0:T(8,128)(2,1)S(1)} %bitcast.72, bf16[2,768,1792]{2,1,0:T(8,128)(2,1)S(1)} %maximum_select_fusion.1), kind=kOutput, calls=%fused_computation.5 | convolution fusion | flops 7051018240 | bytes 15859712 | tf_op jit(solution)/shard_map/dot_general | solution.py:18
  567.5 12.4 %fusion.5 = f32[768,2560]{1,0:T(8,128)S(1)} fusion(bf16[1,1792,2560]{2,1,0:T(8,128)(2,1)} %param.9, bf16[384,1792]{1,0:T(8,128)(2,1)S(1)} %bitcast.74, bf16[384,1792]{1,0:T(8,128)(2,1)} %bitcast.76, pred[]{:T(512)S(6)} %eq.10), kind=kOutput, calls=%fused_computation.10 | convolution fusion | flops 7058817024 | bytes 19791872 | tf_op jit(solution)/shard_map/dot_general | solution.py:107
  581.5 2.4 copy-done.6
  584.0 13.3 %fusion.7 = f32[768,2560]{1,0:T(8,128)} fusion(bf16[1,2560,1792]{2,1,0:T(8,128)(2,1)} %param.8, bf16[2,768,1792]{2,1,0:T(8,128)(2,1)S(1)} %copy-done.6), kind=kOutput, calls=%fused_computation.12 | convolution fusion | flops 7046430720 | bytes 19791872 | tf_op jit(solution)/shard_map/dot_general | solution.py:24
  597.3 13.6 %fusion.15 = f32[768,2560]{1,0:T(8,128)S(1)} fusion(f32[768,2560]{1,0:T(8,128)} %fusion.7, bf16[1,2560,1792]{2,1,0:T(8,128)(2,1)} %param.7, bf16[2,768,1792]{2,1,0:T(8,128)(2,1)} %copy-done.5), kind=kOutput, calls=%fused_computation.21 | convolution fusion | flops 7048396800 | bytes 27656192 | tf_op jit(solution)/shard_map/dot_general | solution.py:24
  611.4 16.0 %collective-permute-done.4 = bf16[384,2560]{1,0:T(8,128)(2,1)S(1)} collective-permute-done((bf16[384,2560]{1,0:T(8,128)(2,1)}, bf16[384,2560]{1,0:T(8,128)(2,1)S(1)}, u32[]{:S(2)}, u32[]{:S(2)}) %collective-permute-start.4) | collective-permute-done | bytes 1966112 | tf_op jit(solution)/shard_map/ppermute | solution.py:14
  629.4 38.0 %collective-permute-done.8 = bf16[384,2560]{1,0:T(8,128)(2,1)S(1)} collective-permute-done((bf16[384,2560]{1,0:T(8,128)(2,1)S(1)}, bf16[384,2560]{1,0:T(8,128)(2,1)S(1)}, u32[]{:S(2)}, u32[]{:S(2)}) %collective-permute-start.8) | collective-permute-done | bytes 1966112 | tf_op jit(solution)/shard_map/ppermute | solution.py:14
  670.3 19.9 %collective-permute-done.9 = bf16[192,2560]{1,0:T(8,128)(2,1)S(1)} collective-permute-done((bf16[192,2560]{1,0:T(8,128)(2,1)S(1)}, bf16[192,2560]{1,0:T(8,128)(2,1)S(1)}, u32[]{:S(2)}, u32[]{:S(2)}) %collective-permute-start.9) | collective-permute-done | bytes 983072 | tf_op jit(solution)/shard_map/ppermute | solution.py:14
  691.7 7.8 %copy.13 = bf16[1,2560,1792]{2,1,0:T(8,128)(2,1)} copy(bf16[1,2560,1792]{2,1,0:T(8,128)(2,1)} %get-tuple-element.13) | data formatting | bytes 18350080
  699.5 7.8 %copy.14 = bf16[1,2560,1792]{2,1,0:T(8,128)(2,1)} copy(bf16[1,2560,1792]{2,1,0:T(8,128)(2,1)} %get-tuple-element.14) | data formatting | bytes 18350080
  707.4 7.9 %copy.15 = bf16[1,1792,2560]{2,1,0:T(8,128)(2,1)} copy(bf16[1,1792,2560]{2,1,0:T(8,128)(2,1)} %get-tuple-element.15) | data formatting | bytes 18350080
  (45 shorter events, 12.7 us)
Async XLA Ops:
  7.2 49.3 %copy-start.2 = (bf16[1,1,192,2560]{3,2,1,0:T(8,128)(2,1)S(1)}, bf16[1,1,192,2560]{3,2,1,0:T(8,128)(2,1)}, u32[]{:S(2)}) copy-start(bf16[1,1,192,2560]{3,2,1,0:T(8,128)(2,1)} %param.6) | copy-start | bytes 2949124
  7.2 49.3 %copy-start = (bf16[1,1,192,2560]{3,2,1,0:T(8,128)(2,1)S(1)}, bf16[1,1,192,2560]{3,2,1,0:T(8,128)(2,1)}, u32[]{:S(2)}) copy-start(bf16[1,1,192,2560]{3,2,1,0:T(8,128)(2,1)} %param.5) | copy-start | bytes 2949124
  7.2 684.5 %all-reduce.3.cloned.1.call-start = ((), (), s32[]{:S(2)}) async-start(), calls=%async_computation | async-start | bytes 55050240 | tf_op jit(solution)/shard_map/psum | solution.py:127
  10.3 46.1 %collective-permute-start = (bf16[2,192,2560]{2,1,0:T(8,128)(2,1)}, bf16[2,192,2560]{2,1,0:T(8,128)(2,1)}, u32[]{:S(2)}, u32[]{:S(2)}) collective-permute-start(bf16[2,192,2560]{2,1,0:T(8,128)(2,1)} %pad_maximum_fusion.2), channel_id=1, source_target_pairs={{0,2},{2,0},{4,6},{6,4},{8,10},{10,8},{12,14},{14,12},{1,3},{3,1},... | collective-permute-start | bytes 5898248 | tf_op jit(solution)/shard_map/ppermute | solution.py:14
  60.4 86.4 %collective-permute-start.1 = (bf16[2,384,2560]{2,1,0:T(8,128)(2,1)}, bf16[2,384,2560]{2,1,0:T(8,128)(2,1)}, u32[]{:S(2)}, u32[]{:S(2)}) collective-permute-start(bf16[2,384,2560]{2,1,0:T(8,128)(2,1)} %maximum_select_fusion.2), channel_id=1, source_target_pairs={{0,4},{4,0},{2,6},{6,2},{8,12},{12,8},{10,14},{14,10},{1,5},{5,1},... | collective-permute-start | bytes 11796488 | tf_op jit(solution)/shard_map/ppermute | solution.py:14
  153.6 13.7 %copy-start.4 = (bf16[2,768,2560]{2,1,0:T(8,128)(2,1)}, bf16[2,768,2560]{2,1,0:T(8,128)(2,1)S(1)}, u32[]{:S(2)}) copy-start(bf16[2,768,2560]{2,1,0:T(8,128)(2,1)S(1)} %maximum_select_fusion) | copy-start | bytes 23592964
  180.1 150.5 %collective-permute-start.2 = (bf16[2,384,1792]{2,1,0:T(8,128)(2,1)}, bf16[2,384,1792]{2,1,0:T(8,128)(2,1)}, u32[]{:S(2)}, u32[]{:S(2)}) collective-permute-start(bf16[2,384,1792]{2,1,0:T(8,128)(2,1)} %select_convert_fusion), channel_id=1, source_target_pairs={{0,8},{8,0},{2,10},{10,2},{4,12},{12,4},{6,14},{14,6},{1,9},{9,1},... | collective-permute-start | bytes 8257544 | tf_op jit(solution)/shard_map/ppermute | solution.py:14
  193.6 165.6 %collective-permute-start.6 = (bf16[1,384,1792]{2,1,0:T(8,128)(2,1)S(1)}, bf16[1,384,1792]{2,1,0:T(8,128)(2,1)S(1)}, u32[]{:S(2)}, u32[]{:S(2)}) collective-permute-start(bf16[1,384,1792]{2,1,0:T(8,128)(2,1)S(1)} %select_convert_fusion.3), channel_id=1, source_target_pairs={{0,8},{8,0},{2,10},{10,2},{4,12},{12,4},{6,14},{14,6},{1,9},{9,1},... | collective-permute-start | bytes 4128776 | tf_op jit(solution)/shard_map/ppermute | solution.py:14
  361.1 3.3 copy-start.7
  361.1 122.2 %collective-permute-start.3 = (bf16[1,384,1792]{2,1,0:T(8,128)(2,1)S(1)}, bf16[1,384,1792]{2,1,0:T(8,128)(2,1)S(1)}, u32[]{:S(2)}, u32[]{:S(2)}) collective-permute-start(bf16[1,384,1792]{2,1,0:T(8,128)(2,1)S(1)} %get-tuple-element.10), channel_id=1, source_target_pairs={{0,8},{8,0},{2,10},{10,2},{4,12},{12,4},{6,14},{14,6},{1,9},{9,1},... | collective-permute-start | bytes 4128776 | tf_op jit(solution)/shard_map/ppermute | solution.py:14
  361.2 185.1 %slice-start = ((s8[7864320]{0:T(1024)(128)(4,1)}), s8[4194304]{0:T(1024)(128)(4,1)S(1)}, s32[]{:S(2)}) async-start(s8[7864320]{0:T(1024)(128)(4,1)} %bitcast.71), calls=%async_computation.1 | async-start | bytes 8388608
  361.4 179.5 %collective-permute-start.7 = (bf16[2,384,1792]{2,1,0:T(8,128)(2,1)S(1)}, bf16[2,384,1792]{2,1,0:T(8,128)(2,1)S(1)}, u32[]{:S(2)}, u32[]{:S(2)}) collective-permute-start(bf16[2,384,1792]{2,1,0:T(8,128)(2,1)S(1)} %pad_maximum_fusion.1), channel_id=1, source_target_pairs={{0,8},{8,0},{2,10},{10,2},{4,12},{12,4},{6,14},{14,6},{1,9},{9,1},... | collective-permute-start | bytes 8257544 | tf_op jit(solution)/shard_map/ppermute | solution.py:14
  483.2 12.8 %copy-start.9 = (bf16[1,384,1792]{2,1,0:T(8,128)(2,1)}, bf16[1,384,1792]{2,1,0:T(8,128)(2,1)S(1)}, u32[]{:S(2)}) copy-start(bf16[1,384,1792]{2,1,0:T(8,128)(2,1)S(1)} %collective-permute-done.3) | copy-start | bytes 4128772
  483.2 63.0 %slice-start.1 = ((s8[7864320]{0:T(1024)(128)(4,1)}), s8[3670016]{0:T(1024)(128)(4,1)S(1)}, s32[]{:S(2)}) async-start(s8[7864320]{0:T(1024)(128)(4,1)} %bitcast.71), calls=%async_computation.2 | async-start | bytes 7340032
  546.3 10.0 %copy-start.5 = (bf16[2,768,1792]{2,1,0:T(8,128)(2,1)}, bf16[2,768,1792]{2,1,0:T(8,128)(2,1)S(1)}, u32[]{:S(2)}) copy-start(bf16[2,768,1792]{2,1,0:T(8,128)(2,1)S(1)} %maximum_select_fusion.1) | copy-start | bytes 16515076
  566.1 1.3 copy-start.8
  579.9 4.1 copy-start.6
  581.5 45.9 %collective-permute-start.4 = (bf16[384,2560]{1,0:T(8,128)(2,1)}, bf16[384,2560]{1,0:T(8,128)(2,1)S(1)}, u32[]{:S(2)}, u32[]{:S(2)}) collective-permute-start(bf16[384,2560]{1,0:T(8,128)(2,1)} %select_convert_fusion.2), channel_id=1, source_target_pairs={{0,4},{4,0},{2,6},{6,2},{8,12},{12,8},{10,14},{14,10},{1,5},{5,1},... | collective-permute-start | bytes 5898248 | tf_op jit(solution)/shard_map/ppermute | solution.py:14
  611.2 56.2 %collective-permute-start.8 = (bf16[384,2560]{1,0:T(8,128)(2,1)S(1)}, bf16[384,2560]{1,0:T(8,128)(2,1)S(1)}, u32[]{:S(2)}, u32[]{:S(2)}) collective-permute-start(bf16[384,2560]{1,0:T(8,128)(2,1)S(1)} %select_convert_fusion.1), channel_id=1, source_target_pairs={{0,4},{4,0},{2,6},{6,2},{8,12},{12,8},{10,14},{14,10},{1,5},{5,1},... | collective-permute-start | bytes 5898248 | tf_op jit(solution)/shard_map/ppermute | solution.py:14
  628.5 40.3 %copy-start.1 = (bf16[1,1,192,2560]{3,2,1,0:T(8,128)(2,1)S(1)}, bf16[1,1,192,2560]{3,2,1,0:T(8,128)(2,1)}, u32[]{:S(2)}) copy-start(bf16[1,1,192,2560]{3,2,1,0:T(8,128)(2,1)} %param.5) | copy-start | bytes 2949124
  628.5 40.2 %collective-permute-start.5 = (bf16[192,2560]{1,0:T(8,128)(2,1)S(1)}, bf16[192,2560]{1,0:T(8,128)(2,1)S(1)}, u32[]{:S(2)}, u32[]{:S(2)}) collective-permute-start(bf16[192,2560]{1,0:T(8,128)(2,1)S(1)} %select_convert_fusion.5), channel_id=1, source_target_pairs={{0,2},{2,0},{4,6},{6,4},{8,10},{10,8},{12,14},{14,12},{1,3},{3,1},... | collective-permute-start | bytes 2949128 | tf_op jit(solution)/shard_map/ppermute | solution.py:14
  668.5 21.7 %copy-start.3 = (bf16[1,1,192,2560]{3,2,1,0:T(8,128)(2,1)S(1)}, bf16[1,1,192,2560]{3,2,1,0:T(8,128)(2,1)}, u32[]{:S(2)}) copy-start(bf16[1,1,192,2560]{3,2,1,0:T(8,128)(2,1)} %param.6) | copy-start | bytes 2949124
  668.5 21.7 %collective-permute-start.9 = (bf16[192,2560]{1,0:T(8,128)(2,1)S(1)}, bf16[192,2560]{1,0:T(8,128)(2,1)S(1)}, u32[]{:S(2)}, u32[]{:S(2)}) collective-permute-start(bf16[192,2560]{1,0:T(8,128)(2,1)S(1)} %select_convert_fusion.4), channel_id=1, source_target_pairs={{0,2},{2,0},{4,6},{6,4},{8,10},{10,8},{12,14},{14,12},{1,3},{3,1},... | collective-permute-start | bytes 2949128 | tf_op jit(solution)/shard_map/ppermute | solution.py:14
Sparse Core Ops, SparseCore 0:
  566.3 85.2 all-reduce.2
where the time goes:
time: 731 us; the launch traced here: 723 us
  waiting for transfers between devices  528 us (72%)
  matrix products  107 us (15%)
  other arithmetic  33 us (5%)
  local copies, waits for them, and re-layouts  27.4 us (4%)
  between operations  14.7 us (2%)
  starting transfers between devices  12.2 us (2%)
    ppermute x10, waiting for transfers between devices, from_partner(): return lax.ppermute(block, axis, route)  528 us
    dot_general x3, matrix products, contract_cols(): lax.dot_general(left, right, (((1,), (1,)), ((), ())), preferred_element_...  37.5 us
    dot_general x3, matrix products, contract_rows(): lax.dot_general(left, right, (((0,), (0,)), ((), ())), preferred_element_...  32.6 us
    unnamed x27, local copies, waits for them, and re-layouts  27.4 us
    select_n x3, other arithmetic, order_pair(): jnp.where(is_upper, jnp.concatenate([other, mine], 1), jnp.concatenate([m...  16 us
  transfers between devices with their start and end apart: 11, of which 9 were waited for; matrix products, arithmetic and copies ran while one was open for 10% of the time, Pallas kernels for 0%

commit v1 on v0

--- a/solution.py
+++ b/solution.py
@@ -137,9 +137,163 @@
     )
 
 
+def flip_grid(block, mask):
+    count = lax.axis_size("grid")
+    return lax.ppermute(block, "grid", [(i, i ^ mask) for i in range(count)])
+
+
+def flip_dp(block):
+    return lax.ppermute(block, "dp", [(0, 1), (1, 0)])
+
+
+def after(value, *others):
+    return lax.optimization_barrier((value,) + others)[0]
+
+
+def two_row_device(acts, cotangent, w_gate, w_up, w_down):
+    return two_row_body(acts[0, 0], cotangent[0, 0], w_gate[0], w_up[0], w_down[0])
+
+
+def two_row_body(own_acts, own_grads, gate_tile, up_tile, down_tile):
+    half = own_acts.shape[0] // 2
+    is_upper = lax.axis_index("dp") == 1
+    across = 4
+
+    def each(move, pair, *mask):
+        return tuple(move(x, *mask) for x in pair)
+
+    def to_bf16(value):
+        return value.astype(jnp.bfloat16)
+
+    def partial_terms(pair):
+        return (
+            to_bf16(jnp.dot(pair[0], gate_tile, preferred_element_type=jnp.float32)),
+            to_bf16(jnp.dot(pair[0], up_tile, preferred_element_type=jnp.float32)),
+            to_bf16(contract_cols(pair[1], down_tile)),
+        )
+
+    def exchange(terms):
+        return flip_grid(jnp.stack(terms), across)
+
+    def summed(mine, other):
+        return [m.astype(jnp.float32) + other[i].astype(jnp.float32) for i, m in enumerate(mine)]
+
+    def gate_values(gate_pre):
+        sigmoid_g = jax.nn.sigmoid(gate_pre)
+        return sigmoid_g, gate_pre * sigmoid_g
+
+    def hidden_of(gate_pre, up_proj):
+        return to_bf16(gate_values(gate_pre)[1] * up_proj)
+
+    def backs_of(gate_pre, up_proj, hidden_grad):
+        sigmoid_g, activated = gate_values(gate_pre)
+        gate_back = hidden_grad * up_proj * sigmoid_g * (1.0 + gate_pre * (1.0 - sigmoid_g))
+        return to_bf16(gate_back), to_bf16(hidden_grad * activated)
+
+    def out_product(hidden):
+        return jnp.dot(hidden, down_tile, preferred_element_type=jnp.float32)
+
+    def input_product(backs):
+        return contract_cols(backs[0], gate_tile) + contract_cols(backs[1], up_tile)
+
+    def ordered(mine, other):
+        return jnp.concatenate(
+            [jnp.where(is_upper, other, mine), jnp.where(is_upper, mine, other)]
+        )
+
+    def grad_term(left, right, held):
+        term = contract_rows(left, right)
+        if held is not None:
+            term = term + held.astype(jnp.float32)
+        return to_bf16(term)
+
+    def finish(mine, other, pair, pair_dp, held):
+        values = summed(mine, other)
+        hidden = hidden_of(values[0], values[1])
+        backs = backs_of(*values)
+        units = jnp.stack((hidden,) + backs)
+        units_dp = flip_dp(units)
+        parts = jnp.stack([out_product(hidden), input_product(backs)])
+        left = ordered(pair[0], pair_dp[0])
+        right = ordered(pair[1], pair_dp[1])
+        all_units = [ordered(units[i], units_dp[i]) for i in range(3)]
+        held = held or (None, None, None)
+        grads = (
+            grad_term(left, all_units[1], held[0]),
+            grad_term(left, all_units[2], held[1]),
+            grad_term(all_units[0], right, held[2]),
+        )
+        return parts, lax.optimization_barrier(grads)
+
+    own = (own_acts, own_grads)
+    near = each(flip_grid, own, 1)
+    first = (own_acts[:half], own_grads[:half])
+    last = (own_acts[half:], own_grads[half:])
+    terms_a = partial_terms(first)
+    got_a = exchange(terms_a)
+    far = each(flip_grid, after(own, terms_a), 2)
+    own_dp = each(flip_dp, own)
+
+    terms_1 = partial_terms(near)
+    got_1 = exchange(terms_1)
+    near_dp = each(flip_dp, near)
+    corner = each(flip_grid, far, 1)
+    far_dp = each(flip_dp, far)
+    terms_3 = partial_terms(after(corner, terms_1))
+    got_3 = exchange(terms_3)
+    corner_dp = each(flip_dp, corner)
+    terms_2 = partial_terms(after(far, terms_3))
+    got_2 = exchange(terms_2)
+    terms_b = partial_terms(after(last, terms_2))
+    got_b = exchange(terms_b[:2])
+    got_c = exchange(terms_b[2:])
+
+    parts_a, held = finish(terms_a, got_a, first, each(lambda x: x[:half], own_dp), None)
+    parts_1, held = finish(terms_1, got_1, near, near_dp, held)
+    from_near = flip_grid(to_bf16(parts_1), 1)
+    parts_3, held = finish(terms_3, got_3, corner, corner_dp, held)
+    from_side = flip_grid(to_bf16(parts_3), 1)
+    parts_2, held = finish(terms_2, got_2, far, far_dp, held)
+    from_far = flip_grid(to_bf16(parts_2 + from_side.astype(jnp.float32)), 2)
+
+    last_dp = each(lambda x: x[half:], own_dp)
+    gate_pre, up_proj = summed(terms_b[:2], got_b)
+    hidden = hidden_of(gate_pre, up_proj)
+    hidden_dp = flip_dp(hidden)
+    out_b = out_product(hidden)
+    down_grad = grad_term(
+        ordered(hidden, hidden_dp), ordered(last[1], last_dp[1]), held[2]
+    )
+    left = ordered(last[0], last_dp[0])
+    (hidden_grad,) = summed(terms_b[2:], got_c)
+    sums_again = summed(lax.optimization_barrier(terms_b[:2] + (hidden,))[:2], after(got_b, hidden))
+    backs = backs_of(*sums_again, hidden_grad)
+    backs_dp = each(flip_dp, backs)
+    input_b = input_product(backs)
+    gate_grad = grad_term(left, ordered(backs[0], backs_dp[0]), held[0])
+    up_grad = grad_term(left, ordered(backs[1], backs_dp[1]), held[1])
+
+    from_far = after(from_far, input_b)
+    others = from_near.astype(jnp.float32) + from_far.astype(jnp.float32)
+    block_out = to_bf16(
+        own_acts.astype(jnp.float32) + (jnp.concatenate([parts_a[0], out_b]) + others[0])
+    )
+    input_grad = to_bf16(
+        own_grads.astype(jnp.float32) + (jnp.concatenate([parts_a[1], input_b]) + others[1])
+    )
+    return (
+        block_out[None, None],
+        input_grad[None, None],
+        gate_grad[None],
+        up_grad[None],
+        down_grad[None],
+    )
+
+
 def solution(mesh):
+    plan = two_row_device if mesh.shape["grid"] == 8 and mesh.shape["dp"] == 2 else per_device
     return jax.shard_map(
-        per_device,
+        plan,
         mesh=mesh,
         in_specs=(
             P(("groups", "dp"), "grid", None, None),

time: 731 us -> 668 us (0.914)
  waiting for transfers between devices: 528 us -> 290 us
  matrix products: 107 us -> 267 us
  other arithmetic: 33 us -> 71.1 us
  local copies, waits for them, and re-layouts: 27.4 us -> 5.26 us
  between operations: 14.7 us -> 1.7 us
  starting transfers between devices: 12.2 us -> 22.7 us
    ppermute x10 -> x30, waiting for transfers between devices: 528 us -> 290 us  [the longest x15 290 us: flip_grid(): return lax.ppermute(block, 'grid', [(i, i ^ mask) for i in range(count)])]
    dot_general x3 -> x15, matrix products: 32.6 us -> 140 us  [contract_rows(): lax.dot_general(left, right, (((0,), (0,)), ((), ())), preferred_element_...]
    dot_general x3 -> x15, matrix products: 37.5 us -> 74 us  [contract_cols(): lax.dot_general(left, right, (((1,), (1,)), ((), ())), preferred_element_...]
    unnamed x27 -> x170, local copies, waits for them, and re-layouts: 27.4 us -> 4.42 us
    select_n x3 -> x15, other arithmetic: 16 us -> 36.3 us  [ordered(): jnp.where(is_upper, other, mine)]
    dot_general x3 -> x15, matrix products: 37 us -> 53.1 us  [the longest x5 21.7 us: partial_terms(): jnp.dot(pair[0], up_tile, preferred_element_type=jnp.float32)]
    another operation x2 -> x11, other arithmetic: 3.33 us -> 16.3 us  [the longest x5 6.57 us: exchange(): return flip_grid(jnp.stack(terms), across)]
    ppermute x10 -> x30, starting transfers between devices: 12.2 us -> 22.7 us  [the longest x15 19.6 us: flip_grid(): return lax.ppermute(block, 'grid', [(i, i ^ mask) for i in range(count)])]
  transfers between devices with their start and end apart: 11 -> 30, of which waited for: 9 -> 8; matrix products, arithmetic and copies ran while one was open for 10% -> 51% of each run, Pallas kernels for 0% -> 0%
where the time goes in v1:
time: 668 us; the launch traced here: 658 us
  waiting for transfers between devices  290 us (43%)
  matrix products  267 us (40%)
  other arithmetic  71.1 us (11%)
  starting transfers between devices  22.7 us (3%)
    ppermute x15, waiting for transfers between devices, flip_grid(): return lax.ppermute(block, 'grid', [(i, i ^ mask) for i in range(count)])  290 us
    dot_general x15, matrix products, contract_rows(): lax.dot_general(left, right, (((0,), (0,)), ((), ())), preferred_element_...  140 us
    dot_general x15, matrix products, contract_cols(): lax.dot_general(left, right, (((1,), (1,)), ((), ())), preferred_element_...  74 us
    select_n x15, other arithmetic, ordered(): jnp.where(is_upper, other, mine)  36.3 us
    dot_general x5, matrix products, partial_terms(): jnp.dot(pair[0], up_tile, preferred_element_type=jnp.float32)  21.7 us
    ppermute x15, starting transfers between devices, flip_grid(): return lax.ppermute(block, 'grid', [(i, i ^ mask) for i in range(count)])  19.6 us
    dot_general x5, matrix products, partial_terms(): jnp.dot(pair[0], gate_tile, preferred_element_type=jnp.float32)  18.7 us
    convert_element_type x8, other arithmetic, to_bf16(): return value.astype(jnp.bfloat16)  16.3 us
  transfers between devices with their start and end apart: 30, of which 8 were waited for; matrix products, arithmetic and copies ran while one was open for 51% of the time, Pallas kernels for 0%

profile of v1, /device:TPU:0, one launch (start us, length us, event | category | flops | bytes accessed | tf_op | source)
XLA Modules:
  0.0 658.0 jit_solution(5543383761878505826)
XLA Ops:
  4.4 5.7 fusion.145
  19.8 6.8 %collective-permute-done.5 = bf16[192,2560]{1,0:T(8,128)(2,1)} collective-permute-done((bf16[192,2560]{1,0:T(8,128)(2,1)}, bf16[192,2560]{1,0:T(8,128)(2,1)}, u32[]{:S(2)}, u32[]{:S(2)}) %collective-permute-start.5) | collective-permute-done | bytes 983072 | tf_op jit(solution)/shard_map/ppermute | solution.py:142
  28.7 6.0 fusion.118
  38.2 8.6 %collective-permute-done.6 = bf16[192,2560]{1,0:T(8,128)(2,1)} collective-permute-done((bf16[192,2560]{1,0:T(8,128)(2,1)}, bf16[192,2560]{1,0:T(8,128)(2,1)}, u32[]{:S(2)}, u32[]{:S(2)}) %collective-permute-start.6) | collective-permute-done | bytes 983072 | tf_op jit(solution)/shard_map/ppermute | solution.py:142
  61.0 14.6 %collective-permute-done.2 = bf16[192,2560]{1,0:T(8,128)(2,1)} collective-permute-done((bf16[192,2560]{1,0:T(8,128)(2,1)S(1)}, bf16[192,2560]{1,0:T(8,128)(2,1)}, u32[]{:S(2)}, u32[]{:S(2)}) %collective-permute-start.2) | collective-permute-done | bytes 983072 | tf_op jit(solution)/shard_map/ppermute | solution.py:142
  75.6 64.5 %collective-permute-done = bf16[3,96,1792]{2,1,0:T(8,128)(2,1)} collective-permute-done((bf16[3,96,1792]{2,1,0:T(8,128)(2,1)}, bf16[3,96,1792]{2,1,0:T(8,128)(2,1)}, u32[]{:S(2)}, u32[]{:S(2)}) %collective-permute-start) | collective-permute-done | bytes 1032224 | tf_op jit(solution)/shard_map/ppermute | solution.py:142
  154.4 6.4 collective-permute-done.4
  163.7 5.6 fusion.130
  173.3 5.9 fusion.133
  188.9 5.2 fusion.154
  220.4 6.3 convolution_convert_fusion.2
  226.6 7.4 %convolution_convert_fusion.1 = bf16[2560,1792]{1,0:T(8,128)(2,1)} fusion(bf16[96,1792]{1,0:T(8,128)(2,1)S(1)} %copy-done.38, bf16[96,1792]{1,0:T(8,128)(2,1)} %get-tuple-element.128, bf16[96,2560]{1,0:T(8,128)(2,1)S(1)} %get-tuple-element.101, bf16[96,2560]{1,0:T(8,128)(2,1)S(1)} %get-tuple-element.100), kind=kOutput, calls=%fused_computation.13 | convolution fusion | flops 1769537536 | bytes 10846208 | tf_op jit(solution)/shard_map/dot_general | solution.py:18
  234.1 6.2 convolution_convert_fusion
  240.3 181.7 %collective-permute-done.7 = bf16[2,96,1792]{2,1,0:T(8,128)(2,1)S(1)} collective-permute-done((bf16[2,96,1792]{2,1,0:T(8,128)(2,1)}, bf16[2,96,1792]{2,1,0:T(8,128)(2,1)S(1)}, u32[]{:S(2)}, u32[]{:S(2)}) %collective-permute-start.7) | collective-permute-done | bytes 688160 | tf_op jit(solution)/shard_map/ppermute | solution.py:142
  422.6 6.2 collective-permute-done.14
  430.3 6.5 fusion.25
  455.0 8.3 %fusion.31 = f32[192,2560]{1,0:T(8,128)} fusion(bf16[192,1792]{1,0:T(8,128)(2,1)S(1)} %get-tuple-element.57, bf16[1,2560,1792]{2,1,0:T(8,128)(2,1)} %param.8), kind=kOutput, calls=%fused_computation.46 | convolution fusion | flops 1761607680 | bytes 11829248 | tf_op jit(solution)/shard_map/dot_general | solution.py:24
  465.3 5.6 fusion.97
  479.2 8.8 %fusion.27 = f32[192,2560]{1,0:T(8,128)} fusion(bf16[192,1792]{1,0:T(8,128)(2,1)S(1)} %get-tuple-element.60, bf16[1,2560,1792]{2,1,0:T(8,128)(2,1)} %param.8), kind=kOutput, calls=%fused_computation.42 | convolution fusion | flops 1761607680 | bytes 11829248 | tf_op jit(solution)/shard_map/dot_general | solution.py:24
  503.5 6.7 %fusion.29 = f32[192,2560]{1,0:T(8,128)S(1)} fusion(bf16[192,1792]{1,0:T(8,128)(2,1)S(1)} %get-tuple-element.63, bf16[1,2560,1792]{2,1,0:T(8,128)(2,1)} %param.8), kind=kOutput, calls=%fused_computation.44 | convolution fusion | flops 1761607680 | bytes 11829248 | tf_op jit(solution)/shard_map/dot_general | solution.py:24
  521.6 13.6 %add_convert_fusion.11 = bf16[2560,1792]{1,0:T(8,128)(2,1)} fusion(bf16[2560,1792]{1,0:T(8,128)(2,1)} %convolution_convert_fusion.2, bf16[192,1792]{1,0:T(8,128)(2,1)} %get-tuple-element.90, bf16[192,1792]{1,0:T(8,128)(2,1)} %get-tuple-element.91, bf16[192,2560]{1,0:T(8,128)(2,1)} %get-tuple-element.113, bf16[192,2560]{1,0:T(8,128)(2,1)} %get-tuple-element.112), kind=kOutput, calls=%fused_computation.11 | convolution fusion | flops 3543662592 | bytes 21692416 | tf_op jit(solution)/shard_map/dot_general | solution.py:18
  535.2 10.7 %add_convert_fusion.10 = bf16[2560,1792]{1,0:T(8,128)(2,1)} fusion(bf16[2560,1792]{1,0:T(8,128)(2,1)S(1)} %bitcast.457, bf16[192,1792]{1,0:T(8,128)(2,1)} %get-tuple-element.92, bf16[192,1792]{1,0:T(8,128)(2,1)} %get-tuple-element.93, bf16[192,2560]{1,0:T(8,128)(2,1)} %get-tuple-element.113, bf16[192,2560]{1,0:T(8,128)(2,1)} %get-tuple-element.112), kind=kOutput, calls=%fused_computation.10 | convolution fusion | flops 3543662592 | bytes 21692416 | tf_op jit(solution)/shard_map/dot_general | solution.py:18
  545.9 13.8 %add_convert_fusion.9 = bf16[1792,2560]{1,0:T(8,128)(2,1)} fusion(bf16[1792,2560]{1,0:T(8,128)(2,1)} %convolution_convert_fusion, bf16[192,2560]{1,0:T(8,128)(2,1)} %get-tuple-element.111, bf16[192,2560]{1,0:T(8,128)(2,1)} %get-tuple-element.110, bf16[192,1792]{1,0:T(8,128)(2,1)} %get-tuple-element.77, bf16[192,1792]{1,0:T(8,128)(2,1)} %get-tuple-element.76), kind=kOutput, calls=%fused_computation.9 | convolution fusion | flops 3543662592 | bytes 21692416 | tf_op jit(solution)/shard_map/dot_general | solution.py:18
  566.8 10.2 %add_convert_fusion.8 = bf16[2560,1792]{1,0:T(8,128)(2,1)} fusion(bf16[2560,1792]{1,0:T(8,128)(2,1)} %add_convert_fusion.11, bf16[192,1792]{1,0:T(8,128)(2,1)} %get-tuple-element.86, bf16[192,1792]{1,0:T(8,128)(2,1)} %get-tuple-element.87, bf16[192,2560]{1,0:T(8,128)(2,1)S(1)} %copy-done.45, bf16[192,2560]{1,0:T(8,128)(2,1)S(1)} %copy-done.44), kind=kOutput, calls=%fused_computation.8 | convolution fusion | flops 3543662592 | bytes 21692416 | tf_op jit(solution)/shard_map/dot_general | solution.py:18
  577.0 10.1 %add_convert_fusion.6 = bf16[1792,2560]{1,0:T(8,128)(2,1)} fusion(bf16[1792,2560]{1,0:T(8,128)(2,1)} %add_convert_fusion.9, bf16[192,2560]{1,0:T(8,128)(2,1)S(1)} %copy-done.47, bf16[192,2560]{1,0:T(8,128)(2,1)S(1)} %copy-done.46, bf16[192,1792]{1,0:T(8,128)(2,1)} %get-tuple-element.71, bf16[192,1792]{1,0:T(8,128)(2,1)} %get-tuple-element.70), kind=kOutput, calls=%fused_computation.6 | convolution fusion | flops 3543662592 | bytes 21692416 | tf_op jit(solution)/shard_map/dot_general | solution.py:18
  587.1 9.8 %add_convert_fusion.7 = bf16[2560,1792]{1,0:T(8,128)(2,1)} fusion(bf16[2560,1792]{1,0:T(8,128)(2,1)} %add_convert_fusion.10, bf16[192,1792]{1,0:T(8,128)(2,1)S(1)} %copy-done.54, bf16[192,1792]{1,0:T(8,128)(2,1)} %get-tuple-element.89, bf16[192,2560]{1,0:T(8,128)(2,1)S(1)} %copy-done.45, bf16[192,2560]{1,0:T(8,128)(2,1)S(1)} %copy-done.44), kind=kOutput, calls=%fused_computation.7 | convolution fusion | flops 3543662592 | bytes 21692416 | tf_op jit(solution)/shard_map/dot_general | solution.py:18
  600.1 9.8 %add_convert_fusion.5 = bf16[2560,1792]{1,0:T(8,128)(2,1)} fusion(bf16[2560,1792]{1,0:T(8,128)(2,1)} %add_convert_fusion.8, bf16[192,1792]{1,0:T(8,128)(2,1)S(1)} %get-tuple-element.84, bf16[192,1792]{1,0:T(8,128)(2,1)S(1)} %get-tuple-element.85, bf16[192,2560]{1,0:T(8,128)(2,1)S(1)} %copy-done.41, bf16[192,2560]{1,0:T(8,128)(2,1)S(1)} %copy-done.40), kind=kOutput, calls=%fused_computation.5 | convolution fusion | flops 3543662592 | bytes 21692416 | tf_op jit(solution)/shard_map/dot_general | solution.py:18
  609.9 10.0 %add_convert_fusion.4 = bf16[2560,1792]{1,0:T(8,128)(2,1)} fusion(bf16[2560,1792]{1,0:T(8,128)(2,1)} %add_convert_fusion.7, bf16[192,1792]{1,0:T(8,128)(2,1)S(1)} %copy-done.55, bf16[192,1792]{1,0:T(8,128)(2,1)S(1)} %copy-done.56, bf16[192,2560]{1,0:T(8,128)(2,1)S(1)} %copy-done.41, bf16[192,2560]{1,0:T(8,128)(2,1)S(1)} %copy-done.40), kind=kOutput, calls=%fused_computation.4 | convolution fusion | flops 3543662592 | bytes 21692416 | tf_op jit(solution)/shard_map/dot_general | solution.py:18
  619.9 9.9 %add_convert_fusion.3 = bf16[1792,2560]{1,0:T(8,128)(2,1)} fusion(bf16[1792,2560]{1,0:T(8,128)(2,1)} %add_convert_fusion.6, bf16[192,2560]{1,0:T(8,128)(2,1)S(1)} %copy-done.43, bf16[192,2560]{1,0:T(8,128)(2,1)S(1)} %copy-done.42, bf16[192,1792]{1,0:T(8,128)(2,1)S(1)} %copy-done.53, bf16[192,1792]{1,0:T(8,128)(2,1)S(1)} %get-tuple-element.64), kind=kOutput, calls=%fused_computation.3 | convolution fusion | flops 3543662592 | bytes 21692416 | tf_op jit(solution)/shard_map/dot_general | solution.py:18
  629.9 7.4 %fusion = bf16[1,2560,1792]{2,1,0:T(8,128)(2,1)} fusion(bf16[2560,1792]{1,0:T(8,128)(2,1)} %add_convert_fusion.5, bf16[96,1792]{1,0:T(8,128)(2,1)S(1)} %copy-done.62, bf16[96,1792]{1,0:T(8,128)(2,1)S(1)} %copy-done.61, bf16[96,2560]{1,0:T(8,128)(2,1)S(1)} %copy-done.58, bf16[96,2560]{1,0:T(8,128)(2,1)S(1)} %copy-done.57), kind=kOutput, calls=%fused_computation.15 | convolution fusion | flops 1778712576 | bytes 20021248 | tf_op jit(solution)/shard_map/dot_general | solution.py:18
  637.4 7.5 %fusion.1 = bf16[1,2560,1792]{2,1,0:T(8,128)(2,1)} fusion(bf16[2560,1792]{1,0:T(8,128)(2,1)} %add_convert_fusion.4, bf16[96,1792]{1,0:T(8,128)(2,1)S(1)} %copy-done.64, bf16[96,1792]{1,0:T(8,128)(2,1)S(1)} %copy-done.63, bf16[96,2560]{1,0:T(8,128)(2,1)S(1)} %copy-done.58, bf16[96,2560]{1,0:T(8,128)(2,1)S(1)} %copy-done.57), kind=kOutput, calls=%fused_computation.16 | convolution fusion | flops 1778712576 | bytes 20021248 | tf_op jit(solution)/shard_map/dot_general | solution.py:18
  644.9 7.4 %fusion.2 = bf16[1,1792,2560]{2,1,0:T(8,128)(2,1)} fusion(bf16[1792,2560]{1,0:T(8,128)(2,1)} %add_convert_fusion.3, bf16[96,2560]{1,0:T(8,128)(2,1)S(1)} %copy-done.60, bf16[96,2560]{1,0:T(8,128)(2,1)S(1)} %copy-done.59, bf16[96,1792]{1,0:T(8,128)(2,1)S(1)} %copy-done.66, bf16[96,1792]{1,0:T(8,128)(2,1)S(1)} %copy-done.65), kind=kOutput, calls=%fused_computation.17 | convolution fusion | flops 1778712576 | bytes 20021248 | tf_op jit(solution)/shard_map/dot_general | solution.py:18
  (286 shorter events, 163.1 us)
Async XLA Ops:
  0.6 26.0 %collective-permute-start.5 = (bf16[192,2560]{1,0:T(8,128)(2,1)}, bf16[192,2560]{1,0:T(8,128)(2,1)}, u32[]{:S(2)}, u32[]{:S(2)}) collective-permute-start(bf16[192,2560]{1,0:T(8,128)(2,1)} %bitcast.453), channel_id=1, source_target_pairs={{0,2},{2,0},{4,6},{6,4},{8,10},{10,8},{12,14},{14,12},{1,3},{3,1},... | collective-permute-start | bytes 2949128 | tf_op jit(solution)/shard_map/ppermute | solution.py:142
  3.7 51.8 %collective-permute-start.15 = (bf16[192,2560]{1,0:T(8,128)(2,1)}, bf16[192,2560]{1,0:T(8,128)(2,1)}, u32[]{:S(2)}, u32[]{:S(2)}) collective-permute-start(bf16[192,2560]{1,0:T(8,128)(2,1)} %bitcast.454), channel_id=1, source_target_pairs={{0,1},{1,0},{2,3},{3,2},{4,5},{5,4},{6,7},{7,6},{8,9},{9,8},{10,11... | collective-permute-start | bytes 2949128 | tf_op jit(solution)/shard_map/ppermute | solution.py:146
  3.7 43.1 %collective-permute-start.6 = (bf16[192,2560]{1,0:T(8,128)(2,1)}, bf16[192,2560]{1,0:T(8,128)(2,1)}, u32[]{:S(2)}, u32[]{:S(2)}) collective-permute-start(bf16[192,2560]{1,0:T(8,128)(2,1)} %bitcast.459), channel_id=1, source_target_pairs={{0,2},{2,0},{4,6},{6,4},{8,10},{10,8},{12,14},{14,12},{1,3},{3,1},... | collective-permute-start | bytes 2949128 | tf_op jit(solution)/shard_map/ppermute | solution.py:142
  3.9 54.0 %collective-permute-start.24 = (bf16[192,2560]{1,0:T(8,128)(2,1)}, bf16[192,2560]{1,0:T(8,128)(2,1)}, u32[]{:S(2)}, u32[]{:S(2)}) collective-permute-start(bf16[192,2560]{1,0:T(8,128)(2,1)} %bitcast.460), channel_id=1, source_target_pairs={{0,1},{1,0},{2,3},{3,2},{4,5},{5,4},{6,7},{7,6},{8,9},{9,8},{10,11... | collective-permute-start | bytes 2949128 | tf_op jit(solution)/shard_map/ppermute | solution.py:146
  16.3 44.2 %collective-permute-start.1 = (bf16[192,2560]{1,0:T(8,128)(2,1)S(1)}, bf16[192,2560]{1,0:T(8,128)(2,1)}, u32[]{:S(2)}, u32[]{:S(2)}) collective-permute-start(bf16[192,2560]{1,0:T(8,128)(2,1)S(1)} %bitcast.455), channel_id=1, source_target_pairs={{0,4},{2,6},{4,0},{6,2},{8,12},{10,14},{12,8},{14,10},{1,5},{3,7},... | collective-permute-start | bytes 2949128 | tf_op jit(solution)/shard_map/ppermute | solution.py:142
  26.6 48.9 %collective-permute-start.2 = (bf16[192,2560]{1,0:T(8,128)(2,1)S(1)}, bf16[192,2560]{1,0:T(8,128)(2,1)}, u32[]{:S(2)}, u32[]{:S(2)}) collective-permute-start(bf16[192,2560]{1,0:T(8,128)(2,1)S(1)} %bitcast.461), channel_id=1, source_target_pairs={{0,4},{2,6},{4,0},{6,2},{8,12},{10,14},{12,8},{14,10},{1,5},{3,7},... | collective-permute-start | bytes 2949128 | tf_op jit(solution)/shard_map/ppermute | solution.py:142
  46.8 93.3 %collective-permute-start = (bf16[3,96,1792]{2,1,0:T(8,128)(2,1)}, bf16[3,96,1792]{2,1,0:T(8,128)(2,1)}, u32[]{:S(2)}, u32[]{:S(2)}) collective-permute-start(bf16[3,96,1792]{2,1,0:T(8,128)(2,1)} %pad_maximum_fusion.17), channel_id=1, source_target_pairs={{0,8},{2,10},{4,12},{6,14},{8,0},{10,2},{12,4},{14,6},{1,9},{3,11}... | collective-permute-start | bytes 3096584 | tf_op jit(solution)/shard_map/ppermute | solution.py:142
  55.5 396.9 %collective-permute-start.8 = (bf16[3,192,1792]{2,1,0:T(8,128)(2,1)}, bf16[3,192,1792]{2,1,0:T(8,128)(2,1)}, u32[]{:S(2)}, u32[]{:S(2)}) collective-permute-start(bf16[3,192,1792]{2,1,0:T(8,128)(2,1)} %pad_maximum_fusion), channel_id=1, source_target_pairs={{0,8},{2,10},{4,12},{6,14},{8,0},{10,2},{12,4},{14,6},{1,9},{3,11}... | collective-permute-start | bytes 6193160 | tf_op jit(solution)/shard_map/ppermute | solution.py:142
  57.9 140.6 %collective-permute-start.21 = (bf16[192,2560]{1,0:T(8,128)(2,1)}, bf16[192,2560]{1,0:T(8,128)(2,1)}, u32[]{:S(2)}, u32[]{:S(2)}) collective-permute-start(bf16[192,2560]{1,0:T(8,128)(2,1)} %collective-permute-done.5), channel_id=1, source_target_pairs={{0,1},{1,0},{2,3},{3,2},{4,5},{5,4},{6,7},{7,6},{8,9},{9,8},{10,11... | collective-permute-start | bytes 2949128 | tf_op jit(solution)/shard_map/ppermute | solution.py:146
  60.4 143.2 %collective-permute-start.25 = (bf16[192,2560]{1,0:T(8,128)(2,1)}, bf16[192,2560]{1,0:T(8,128)(2,1)}, u32[]{:S(2)}, u32[]{:S(2)}) collective-permute-start(bf16[192,2560]{1,0:T(8,128)(2,1)} %collective-permute-done.6), channel_id=1, source_target_pairs={{0,1},{1,0},{2,3},{3,2},{4,5},{5,4},{6,7},{7,6},{8,9},{9,8},{10,11... | collective-permute-start | bytes 2949128 | tf_op jit(solution)/shard_map/ppermute | solution.py:146
  75.6 78.8 %collective-permute-start.3 = (bf16[192,2560]{1,0:T(8,128)(2,1)}, bf16[192,2560]{1,0:T(8,128)(2,1)S(1)}, u32[]{:S(2)}, u32[]{:S(2)}) collective-permute-start(bf16[192,2560]{1,0:T(8,128)(2,1)} %collective-permute-done.1), channel_id=1, source_target_pairs={{0,2},{2,0},{4,6},{6,4},{8,10},{10,8},{12,14},{14,12},{1,3},{3,1},... | collective-permute-start | bytes 2949128 | tf_op jit(solution)/shard_map/ppermute | solution.py:142
  140.1 20.7 %collective-permute-start.4 = (bf16[192,2560]{1,0:T(8,128)(2,1)}, bf16[192,2560]{1,0:T(8,128)(2,1)S(1)}, u32[]{:S(2)}, u32[]{:S(2)}) collective-permute-start(bf16[192,2560]{1,0:T(8,128)(2,1)} %collective-permute-done.2), channel_id=1, source_target_pairs={{0,2},{2,0},{4,6},{6,4},{8,10},{10,8},{12,14},{14,12},{1,3},{3,1},... | collective-permute-start | bytes 2949128 | tf_op jit(solution)/shard_map/ppermute | solution.py:142
  154.4 52.1 %collective-permute-start.17 = (bf16[192,2560]{1,0:T(8,128)(2,1)}, bf16[192,2560]{1,0:T(8,128)(2,1)}, u32[]{:S(2)}, u32[]{:S(2)}) collective-permute-start(bf16[192,2560]{1,0:T(8,128)(2,1)} %collective-permute-done.1), channel_id=1, source_target_pairs={{0,1},{1,0},{2,3},{3,2},{4,5},{5,4},{6,7},{7,6},{8,9},{9,8},{10,11... | collective-permute-start | bytes 2949128 | tf_op jit(solution)/shard_map/ppermute | solution.py:146
  161.7 51.6 %collective-permute-start.27 = (bf16[192,2560]{1,0:T(8,128)(2,1)}, bf16[192,2560]{1,0:T(8,128)(2,1)}, u32[]{:S(2)}, u32[]{:S(2)}) collective-permute-start(bf16[192,2560]{1,0:T(8,128)(2,1)} %collective-permute-done.2), channel_id=1, source_target_pairs={{0,1},{1,0},{2,3},{3,2},{4,5},{5,4},{6,7},{7,6},{8,9},{9,8},{10,11... | collective-permute-start | bytes 2949128 | tf_op jit(solution)/shard_map/ppermute | solution.py:146
  198.6 17.7 %collective-permute-start.23 = (bf16[3,96,1792]{2,1,0:T(8,128)(2,1)S(1)}, bf16[3,96,1792]{2,1,0:T(8,128)(2,1)S(1)}, u32[]{:S(2)}, u32[]{:S(2)}) collective-permute-start(bf16[3,96,1792]{2,1,0:T(8,128)(2,1)S(1)} %copy-done.39), channel_id=1, source_target_pairs={{0,1},{1,0},{2,3},{3,2},{4,5},{5,4},{6,7},{7,6},{8,9},{9,8},{10,11... | collective-permute-start | bytes 3096584 | tf_op jit(solution)/shard_map/ppermute | solution.py:146
  203.6 295.1 %collective-permute-start.10 = (bf16[3,192,1792]{2,1,0:T(8,128)(2,1)}, bf16[3,192,1792]{2,1,0:T(8,128)(2,1)}, u32[]{:S(2)}, u32[]{:S(2)}) collective-permute-start(bf16[3,192,1792]{2,1,0:T(8,128)(2,1)} %pad_maximum_fusion.1), channel_id=1, source_target_pairs={{0,8},{2,10},{4,12},{6,14},{8,0},{10,2},{12,4},{14,6},{1,9},{3,11}... | collective-permute-start | bytes 6193160 | tf_op jit(solution)/shard_map/ppermute | solution.py:142
  206.5 269.7 %collective-permute-start.11 = (bf16[3,192,1792]{2,1,0:T(8,128)(2,1)}, bf16[3,192,1792]{2,1,0:T(8,128)(2,1)}, u32[]{:S(2)}, u32[]{:S(2)}) collective-permute-start(bf16[3,192,1792]{2,1,0:T(8,128)(2,1)} %pad_maximum_fusion.2), channel_id=1, source_target_pairs={{0,8},{2,10},{4,12},{6,14},{8,0},{10,2},{12,4},{14,6},{1,9},{3,11}... | collective-permute-start | bytes 6193160 | tf_op jit(solution)/shard_map/ppermute | solution.py:142
  213.3 208.7 %collective-permute-start.7 = (bf16[2,96,1792]{2,1,0:T(8,128)(2,1)}, bf16[2,96,1792]{2,1,0:T(8,128)(2,1)S(1)}, u32[]{:S(2)}, u32[]{:S(2)}) collective-permute-start(bf16[2,96,1792]{2,1,0:T(8,128)(2,1)} %pad_maximum_fusion.21), channel_id=1, source_target_pairs={{0,8},{2,10},{4,12},{6,14},{8,0},{10,2},{12,4},{14,6},{1,9},{3,11}... | collective-permute-start | bytes 2064392 | tf_op jit(solution)/shard_map/ppermute | solution.py:142
  216.2 212.6 %collective-permute-start.14 = (bf16[1,96,1792]{2,1,0:T(8,128)(2,1)S(1)}, bf16[1,96,1792]{2,1,0:T(8,128)(2,1)}, u32[]{:S(2)}, u32[]{:S(2)}) collective-permute-start(bf16[1,96,1792]{2,1,0:T(8,128)(2,1)S(1)} %bitcast.488), channel_id=1, source_target_pairs={{0,8},{2,10},{4,12},{6,14},{8,0},{10,2},{12,4},{14,6},{1,9},{3,11}... | collective-permute-start | bytes 1032200 | tf_op jit(solution)/shard_map/ppermute | solution.py:142
  234.0 194.8 %copy-start.50 = (bf16[192,2560]{1,0:T(8,128)(2,1)S(1)}, bf16[192,2560]{1,0:T(8,128)(2,1)}, u32[]{:S(2)}) copy-start(bf16[192,2560]{1,0:T(8,128)(2,1)} %copy-done.48) | copy-start | bytes 2949124
  234.1 194.8 %copy-start.35 = (bf16[96,1792]{1,0:T(8,128)(2,1)S(1)}, bf16[96,1792]{1,0:T(8,128)(2,1)}, u32[]{:S(2)}) copy-start(bf16[96,1792]{1,0:T(8,128)(2,1)} %copy-done.34) | copy-start | bytes 1032196
  422.1 21.1 %collective-permute-start.19 = (bf16[192,2560]{1,0:T(8,128)(2,1)}, bf16[192,2560]{1,0:T(8,128)(2,1)}, u32[]{:S(2)}, u32[]{:S(2)}) collective-permute-start(bf16[192,2560]{1,0:T(8,128)(2,1)} %copy-done.51), channel_id=1, source_target_pairs={{0,1},{1,0},{2,3},{3,2},{4,5},{5,4},{6,7},{7,6},{8,9},{9,8},{10,11... | collective-permute-start | bytes 2949128 | tf_op jit(solution)/shard_map/ppermute | solution.py:146
  428.8 17.5 %collective-permute-start.26 = (bf16[192,2560]{1,0:T(8,128)(2,1)S(1)}, bf16[192,2560]{1,0:T(8,128)(2,1)}, u32[]{:S(2)}, u32[]{:S(2)}) collective-permute-start(bf16[192,2560]{1,0:T(8,128)(2,1)S(1)} %copy-done.50), channel_id=1, source_target_pairs={{0,1},{1,0},{2,3},{3,2},{4,5},{5,4},{6,7},{7,6},{8,9},{9,8},{10,11... | collective-permute-start | bytes 2949128 | tf_op jit(solution)/shard_map/ppermute | solution.py:146
  443.2 5.8 collective-permute-start.16
  446.3 4.2 collective-permute-start.28
  449.0 2.5 collective-permute-start.29
  473.5 178.8 %collective-permute-start.9 = (bf16[2,192,2560]{2,1,0:T(8,128)(2,1)}, bf16[2,192,2560]{2,1,0:T(8,128)(2,1)}, u32[]{:S(2)}, u32[]{:S(2)}) collective-permute-start(bf16[2,192,2560]{2,1,0:T(8,128)(2,1)} %pad_maximum_fusion.6), channel_id=1, source_target_pairs={{0,2},{2,0},{4,6},{6,4},{8,10},{10,8},{12,14},{14,12},{1,3},{3,1},... | collective-permute-start | bytes 5898248 | tf_op jit(solution)/shard_map/ppermute | solution.py:142
  476.2 41.6 %collective-permute-start.22 = (bf16[3,192,1792]{2,1,0:T(8,128)(2,1)}, bf16[3,192,1792]{2,1,0:T(8,128)(2,1)}, u32[]{:S(2)}, u32[]{:S(2)}) collective-permute-start(bf16[3,192,1792]{2,1,0:T(8,128)(2,1)} %pad_maximum_fusion.5), channel_id=1, source_target_pairs={{0,1},{1,0},{2,3},{3,2},{4,5},{5,4},{6,7},{7,6},{8,9},{9,8},{10,11... | collective-permute-start | bytes 6193160 | tf_op jit(solution)/shard_map/ppermute | solution.py:146
  496.1 64.7 %collective-permute-start.12 = (bf16[2,192,2560]{2,1,0:T(8,128)(2,1)}, bf16[2,192,2560]{2,1,0:T(8,128)(2,1)}, u32[]{:S(2)}, u32[]{:S(2)}) collective-permute-start(bf16[2,192,2560]{2,1,0:T(8,128)(2,1)} %pad_maximum_fusion.7), channel_id=1, source_target_pairs={{0,2},{2,0},{4,6},{6,4},{8,10},{10,8},{12,14},{14,12},{1,3},{3,1},... | collective-permute-start | bytes 5898248 | tf_op jit(solution)/shard_map/ppermute | solution.py:142
  498.5 64.5 %collective-permute-start.20 = (bf16[3,192,1792]{2,1,0:T(8,128)(2,1)}, bf16[3,192,1792]{2,1,0:T(8,128)(2,1)}, u32[]{:S(2)}, u32[]{:S(2)}) collective-permute-start(bf16[3,192,1792]{2,1,0:T(8,128)(2,1)} %pad_maximum_fusion.4), channel_id=1, source_target_pairs={{0,1},{1,0},{2,3},{3,2},{4,5},{5,4},{6,7},{7,6},{8,9},{9,8},{10,11... | collective-permute-start | bytes 6193160 | tf_op jit(solution)/shard_map/ppermute | solution.py:146
  503.3 93.6 %collective-permute-start.18 = (bf16[3,192,1792]{2,1,0:T(8,128)(2,1)}, bf16[3,192,1792]{2,1,0:T(8,128)(2,1)}, u32[]{:S(2)}, u32[]{:S(2)}) collective-permute-start(bf16[3,192,1792]{2,1,0:T(8,128)(2,1)} %pad_maximum_fusion.3), channel_id=1, source_target_pairs={{0,1},{1,0},{2,3},{3,2},{4,5},{5,4},{6,7},{7,6},{8,9},{9,8},{10,11... | collective-permute-start | bytes 6193160 | tf_op jit(solution)/shard_map/ppermute | solution.py:146
  562.9 89.3 %collective-permute-start.13 = (bf16[2,192,2560]{2,1,0:T(8,128)(2,1)S(1)}, bf16[2,192,2560]{2,1,0:T(8,128)(2,1)S(1)}, u32[]{:S(2)}, u32[]{:S(2)}) collective-permute-start(bf16[2,192,2560]{2,1,0:T(8,128)(2,1)S(1)} %fusion.63), channel_id=1, source_target_pairs={{0,4},{2,6},{4,0},{6,2},{8,12},{10,14},{12,8},{14,10},{1,5},{3,7},... | collective-permute-start | bytes 5898248 | tf_op jit(solution)/shard_map/ppermute | solution.py:142
  (83 other events, 685.1 us)

commit v2 on v1

--- a/solution.py
+++ b/solution.py
@@ -196,10 +196,11 @@
     def input_product(backs):
         return contract_cols(backs[0], gate_tile) + contract_cols(backs[1], up_tile)
 
-    def ordered(mine, other):
-        return jnp.concatenate(
-            [jnp.where(is_upper, other, mine), jnp.where(is_upper, mine, other)]
-        )
+    def ordered(*both):
+        rows = []
+        for mine, other in both:
+            rows += [jnp.where(is_upper, other, mine), jnp.where(is_upper, mine, other)]
+        return jnp.concatenate(rows)
 
     def grad_term(left, right, held):
         term = contract_rows(left, right)
@@ -207,23 +208,25 @@
             term = term + held.astype(jnp.float32)
         return to_bf16(term)
 
-    def finish(mine, other, pair, pair_dp, held):
+    def finish(mine, other):
         values = summed(mine, other)
         hidden = hidden_of(values[0], values[1])
         backs = backs_of(*values)
         units = jnp.stack((hidden,) + backs)
         units_dp = flip_dp(units)
         parts = jnp.stack([out_product(hidden), input_product(backs)])
-        left = ordered(pair[0], pair_dp[0])
-        right = ordered(pair[1], pair_dp[1])
-        all_units = [ordered(units[i], units_dp[i]) for i in range(3)]
-        held = held or (None, None, None)
+        return parts, [(units[i], units_dp[i]) for i in range(3)]
+
+    def weight_grads(pieces, held):
+        left = ordered(*((pair[0], pair_dp[0]) for pair, pair_dp, _ in pieces))
+        right = ordered(*((pair[1], pair_dp[1]) for pair, pair_dp, _ in pieces))
+        units = [ordered(*(piece[2][i] for piece in pieces)) for i in range(3)]
         grads = (
-            grad_term(left, all_units[1], held[0]),
-            grad_term(left, all_units[2], held[1]),
-            grad_term(all_units[0], right, held[2]),
+            grad_term(left, units[1], held[0]),
+            grad_term(left, units[2], held[1]),
+            grad_term(units[0], right, held[2]),
         )
-        return parts, lax.optimization_barrier(grads)
+        return lax.optimization_barrier(grads)
 
     own = (own_acts, own_grads)
     near = each(flip_grid, own, 1)
@@ -248,12 +251,15 @@
     got_b = exchange(terms_b[:2])
     got_c = exchange(terms_b[2:])
 
-    parts_a, held = finish(terms_a, got_a, first, each(lambda x: x[:half], own_dp), None)
-    parts_1, held = finish(terms_1, got_1, near, near_dp, held)
+    first_dp = each(lambda x: x[:half], own_dp)
+    parts_a, units_a = finish(terms_a, got_a)
+    parts_1, units_1 = finish(terms_1, got_1)
     from_near = flip_grid(to_bf16(parts_1), 1)
-    parts_3, held = finish(terms_3, got_3, corner, corner_dp, held)
+    held = weight_grads(((first, first_dp, units_a), (near, near_dp, units_1)), (None, None, None))
+    parts_3, units_3 = finish(terms_3, got_3)
     from_side = flip_grid(to_bf16(parts_3), 1)
-    parts_2, held = finish(terms_2, got_2, far, far_dp, held)
+    held = weight_grads(((corner, corner_dp, units_3),), held)
+    parts_2, units_2 = finish(terms_2, got_2)
     from_far = flip_grid(to_bf16(parts_2 + from_side.astype(jnp.float32)), 2)
 
     last_dp = each(lambda x: x[half:], own_dp)
@@ -262,16 +268,18 @@
     hidden_dp = flip_dp(hidden)
     out_b = out_product(hidden)
     down_grad = grad_term(
-        ordered(hidden, hidden_dp), ordered(last[1], last_dp[1]), held[2]
-    )
-    left = ordered(last[0], last_dp[0])
+        ordered(units_2[0], (hidden, hidden_dp)),
+        ordered((far[1], far_dp[1]), (last[1], last_dp[1])),
+        held[2],
+    )
+    left = ordered((far[0], far_dp[0]), (last[0], last_dp[0]))
     (hidden_grad,) = summed(terms_b[2:], got_c)
     sums_again = summed(lax.optimization_barrier(terms_b[:2] + (hidden,))[:2], after(got_b, hidden))
     backs = backs_of(*sums_again, hidden_grad)
     backs_dp = each(flip_dp, backs)
     input_b = input_product(backs)
-    gate_grad = grad_term(left, ordered(backs[0], backs_dp[0]), held[0])
-    up_grad = grad_term(left, ordered(backs[1], backs_dp[1]), held[1])
+    gate_grad = grad_term(left, ordered(units_2[1], (backs[0], backs_dp[0])), held[0])
+    up_grad = grad_term(left, ordered(units_2[2], (backs[1], backs_dp[1])), held[1])
 
     from_far = after(from_far, input_b)
     others = from_near.astype(jnp.float32) + from_far.astype(jnp.float32)
@@ -292,7 +300,7 @@
 
 def solution(mesh):
     plan = two_row_device if mesh.shape["grid"] == 8 and mesh.shape["dp"] == 2 else per_device
-    return jax.shard_map(
+    step = jax.shard_map(
         plan,
         mesh=mesh,
         in_specs=(
@@ -311,3 +319,6 @@
         ),
         check_vma=False,
     )
+    if plan is per_device:
+        return step
+    return step

time: 668 us -> 647 us (0.969)
  matrix products: 267 us -> 226 us
  waiting for transfers between devices: 290 us -> 318 us
  other arithmetic: 71.1 us -> 63.8 us
    dot_general x15 -> x9, matrix products: 140 us -> 97.6 us  [contract_rows(): lax.dot_general(left, right, (((0,), (0,)), ((), ())), preferred_element_...]
    ppermute x15, waiting for transfers between devices: 290 us -> 318 us  [flip_grid(): return lax.ppermute(block, 'grid', [(i, i ^ mask) for i in range(count)])]
  transfers between devices with their start and end apart: 30 -> 30, of which waited for: 8 -> 8; matrix products, arithmetic and copies ran while one was open for 51% -> 45% of each run, Pallas kernels for 0% -> 0%
where the time goes in v2:
time: 647 us; the launch traced here: 637 us
  waiting for transfers between devices  318 us (49%)
  matrix products  226 us (35%)
  other arithmetic  63.8 us (10%)
  starting transfers between devices  22.3 us (3%)
    ppermute x15, waiting for transfers between devices, flip_grid(): return lax.ppermute(block, 'grid', [(i, i ^ mask) for i in range(count)])  318 us
    dot_general x9, matrix products, contract_rows(): lax.dot_general(left, right, (((0,), (0,)), ((), ())), preferred_element_...  97.6 us
    dot_general x15, matrix products, contract_cols(): lax.dot_general(left, right, (((1,), (1,)), ((), ())), preferred_element_...  73.5 us
    select_n x15, other arithmetic, ordered(): rows += [jnp.where(is_upper, other, mine), jnp.where(is_upper, mine, other)]  33.6 us
    dot_general x5, matrix products, partial_terms(): jnp.dot(pair[0], up_tile, preferred_element_type=jnp.float32)  22.4 us
    dot_general x5, matrix products, partial_terms(): jnp.dot(pair[0], gate_tile, preferred_element_type=jnp.float32)  20 us
    ppermute x15, starting transfers between devices, flip_grid(): return lax.ppermute(block, 'grid', [(i, i ^ mask) for i in range(count)])  19.7 us
    convert_element_type x8, other arithmetic, to_bf16(): return value.astype(jnp.bfloat16)  13.6 us
  transfers between devices with their start and end apart: 30, of which 8 were waited for; matrix products, arithmetic and copies ran while one was open for 45% of the time, Pallas kernels for 0%

profile of v2, /device:TPU:0, one launch (start us, length us, event | category | flops | bytes accessed | tf_op | source)
XLA Modules:
  0.0 637.3 jit_solution(4835305114503734589)
XLA Ops:
  4.4 5.7 fusion.159
  19.9 6.8 %collective-permute-done.5 = bf16[192,2560]{1,0:T(8,128)(2,1)} collective-permute-done((bf16[192,2560]{1,0:T(8,128)(2,1)}, bf16[192,2560]{1,0:T(8,128)(2,1)}, u32[]{:S(2)}, u32[]{:S(2)}) %collective-permute-start.5) | collective-permute-done | bytes 983072 | tf_op jit(solution)/shard_map/ppermute | solution.py:142
  28.7 6.0 fusion.132
  38.2 8.6 %collective-permute-done.6 = bf16[192,2560]{1,0:T(8,128)(2,1)} collective-permute-done((bf16[192,2560]{1,0:T(8,128)(2,1)}, bf16[192,2560]{1,0:T(8,128)(2,1)}, u32[]{:S(2)}, u32[]{:S(2)}) %collective-permute-start.6) | collective-permute-done | bytes 983072 | tf_op jit(solution)/shard_map/ppermute | solution.py:142
  49.6 4.3 fusion.150
  61.3 14.2 %collective-permute-done.2 = bf16[192,2560]{1,0:T(8,128)(2,1)} collective-permute-done((bf16[192,2560]{1,0:T(8,128)(2,1)S(1)}, bf16[192,2560]{1,0:T(8,128)(2,1)}, u32[]{:S(2)}, u32[]{:S(2)}) %collective-permute-start.2) | collective-permute-done | bytes 983072 | tf_op jit(solution)/shard_map/ppermute | solution.py:142
  75.6 64.4 %collective-permute-done = bf16[3,96,1792]{2,1,0:T(8,128)(2,1)S(1)} collective-permute-done((bf16[3,96,1792]{2,1,0:T(8,128)(2,1)}, bf16[3,96,1792]{2,1,0:T(8,128)(2,1)S(1)}, u32[]{:S(2)}, u32[]{:S(2)}) %collective-permute-start) | collective-permute-done | bytes 1032224 | tf_op jit(solution)/shard_map/ppermute | solution.py:142
  153.1 7.5 %collective-permute-done.4 = bf16[192,2560]{1,0:T(8,128)(2,1)S(1)} collective-permute-done((bf16[192,2560]{1,0:T(8,128)(2,1)}, bf16[192,2560]{1,0:T(8,128)(2,1)S(1)}, u32[]{:S(2)}, u32[]{:S(2)}) %collective-permute-start.4) | collective-permute-done | bytes 983072 | tf_op jit(solution)/shard_map/ppermute | solution.py:142
  164.8 6.1 fusion.144
  174.0 6.1 fusion.147
  183.5 4.6 fusion.156
  191.4 5.2 fusion.168
  220.2 199.4 %collective-permute-done.7 = bf16[2,96,1792]{2,1,0:T(8,128)(2,1)S(1)} collective-permute-done((bf16[2,96,1792]{2,1,0:T(8,128)(2,1)S(1)}, bf16[2,96,1792]{2,1,0:T(8,128)(2,1)S(1)}, u32[]{:S(2)}, u32[]{:S(2)}) %collective-permute-start.7) | collective-permute-done | bytes 688160 | tf_op jit(solution)/shard_map/ppermute | solution.py:142
  419.9 6.6 %collective-permute-done.14 = bf16[1,96,1792]{2,1,0:T(8,128)(2,1)S(1)} collective-permute-done((bf16[1,96,1792]{2,1,0:T(8,128)(2,1)S(1)}, bf16[1,96,1792]{2,1,0:T(8,128)(2,1)S(1)}, u32[]{:S(2)}, u32[]{:S(2)}) %collective-permute-start.14) | collective-permute-done | bytes 344096 | tf_op jit(solution)/shard_map/ppermute | solution.py:142
  427.0 6.5 %fusion.25 = f32[96,2560]{1,0:T(8,128)S(1)} fusion(bf16[96,1792]{1,0:T(8,128)(2,1)S(1)} %get-tuple-element.106, bf16[1,2560,1792]{2,1,0:T(8,128)(2,1)} %param.8), kind=kOutput, calls=%fused_computation.34 | convolution fusion | flops 880803840 | bytes 10502144 | tf_op jit(solution)/shard_map/dot_general | solution.py:24
  433.5 3.8 fusion.109
  450.5 8.6 %fusion.31 = f32[192,2560]{1,0:T(8,128)} fusion(bf16[192,1792]{1,0:T(8,128)(2,1)S(1)} %get-tuple-element.45, bf16[1,2560,1792]{2,1,0:T(8,128)(2,1)} %param.8), kind=kOutput, calls=%fused_computation.40 | convolution fusion | flops 1761607680 | bytes 11829248 | tf_op jit(solution)/shard_map/dot_general | solution.py:24
  461.1 4.7 fusion.97
  472.5 8.0 %fusion.27 = f32[192,2560]{1,0:T(8,128)} fusion(bf16[192,1792]{1,0:T(8,128)(2,1)S(1)} %get-tuple-element.48, bf16[1,2560,1792]{2,1,0:T(8,128)(2,1)} %param.8), kind=kOutput, calls=%fused_computation.36 | convolution fusion | flops 1761607680 | bytes 11829248 | tf_op jit(solution)/shard_map/dot_general | solution.py:24
  482.5 4.7 fusion.100
  495.7 8.2 %fusion.29 = f32[192,2560]{1,0:T(8,128)} fusion(bf16[192,1792]{1,0:T(8,128)(2,1)S(1)} %get-tuple-element.51, bf16[1,2560,1792]{2,1,0:T(8,128)(2,1)} %param.8), kind=kOutput, calls=%fused_computation.38 | convolution fusion | flops 1761607680 | bytes 11829248 | tf_op jit(solution)/shard_map/dot_general | solution.py:24
  507.2 4.7 fusion.73
  514.5 9.8 %convolution_convert_fusion.1 = bf16[2560,1792]{1,0:T(8,128)(2,1)} fusion(bf16[192,1792]{1,0:T(8,128)(2,1)S(1)} %get-tuple-element.78, bf16[192,1792]{1,0:T(8,128)(2,1)S(1)} %get-tuple-element.79, bf16[96,1792]{1,0:T(8,128)(2,1)S(1)} %copy-done.56, bf16[96,1792]{1,0:T(8,128)(2,1)S(1)} %copy-done.57, bf16[192,2560]{1,0:T(8,128)(2,1)S(1)} %copy-done.36, ...), kind=kOutput, calls=%fused_computation.7 | convolution fusion | flops 5309464576 | bytes 14188544 | tf_op jit(solution)/shard_map/dot_general | solution.py:18
  524.3 9.8 %convolution_convert_fusion = bf16[2560,1792]{1,0:T(8,128)(2,1)} fusion(bf16[192,1792]{1,0:T(8,128)(2,1)S(1)} %get-tuple-element.80, bf16[192,1792]{1,0:T(8,128)(2,1)S(1)} %get-tuple-element.81, bf16[96,1792]{1,0:T(8,128)(2,1)S(1)} %copy-done.54, bf16[96,1792]{1,0:T(8,128)(2,1)S(1)} %copy-done.55, bf16[192,2560]{1,0:T(8,128)(2,1)S(1)} %copy-done.36, ...), kind=kOutput, calls=%fused_computation.6 | convolution fusion | flops 5309464576 | bytes 14188544 | tf_op jit(solution)/shard_map/dot_general | solution.py:18
  534.2 9.8 %convolution_convert_fusion.2 = bf16[1792,2560]{1,0:T(8,128)(2,1)} fusion(bf16[192,2560]{1,0:T(8,128)(2,1)S(1)} %copy-done.38, bf16[192,2560]{1,0:T(8,128)(2,1)S(1)} %copy-done.37, bf16[96,2560]{1,0:T(8,128)(2,1)S(1)} %copy-done.50, bf16[96,2560]{1,0:T(8,128)(2,1)S(1)} %copy-done.49, bf16[192,1792]{1,0:T(8,128)(2,1)S(1)} %get-tuple-element.65, ...), kind=kOutput, calls=%fused_computation.8 | convolution fusion | flops 5309464576 | bytes 14188544 | tf_op jit(solution)/shard_map/dot_general | solution.py:18
  543.9 10.5 %collective-permute-done.12 = bf16[2,192,2560]{2,1,0:T(8,128)(2,1)} collective-permute-done((bf16[2,192,2560]{2,1,0:T(8,128)(2,1)}, bf16[2,192,2560]{2,1,0:T(8,128)(2,1)}, u32[]{:S(2)}, u32[]{:S(2)}) %collective-permute-start.12) | collective-permute-done | bytes 1966112 | tf_op jit(solution)/shard_map/ppermute | solution.py:142
  560.1 10.6 %add_convert_fusion.5 = bf16[2560,1792]{1,0:T(8,128)(2,1)} fusion(bf16[2560,1792]{1,0:T(8,128)(2,1)} %convolution_convert_fusion.1, bf16[192,1792]{1,0:T(8,128)(2,1)} %get-tuple-element.74, bf16[192,1792]{1,0:T(8,128)(2,1)} %get-tuple-element.75, bf16[192,2560]{1,0:T(8,128)(2,1)S(1)} %copy-done.40, bf16[192,2560]{1,0:T(8,128)(2,1)S(1)} %copy-done.39), kind=kOutput, calls=%fused_computation.5 | convolution fusion | flops 3543662592 | bytes 21692416 | tf_op jit(solution)/shard_map/dot_general | solution.py:18
  570.7 10.1 %add_convert_fusion.3 = bf16[1792,2560]{1,0:T(8,128)(2,1)} fusion(bf16[1792,2560]{1,0:T(8,128)(2,1)} %convolution_convert_fusion.2, bf16[192,2560]{1,0:T(8,128)(2,1)S(1)} %copy-done.42, bf16[192,2560]{1,0:T(8,128)(2,1)S(1)} %copy-done.41, bf16[192,1792]{1,0:T(8,128)(2,1)} %get-tuple-element.59, bf16[192,1792]{1,0:T(8,128)(2,1)} %get-tuple-element.58), kind=kOutput, calls=%fused_computation.3 | convolution fusion | flops 3543662592 | bytes 21692416 | tf_op jit(solution)/shard_map/dot_general | solution.py:18
  580.8 9.7 %add_convert_fusion.4 = bf16[2560,1792]{1,0:T(8,128)(2,1)} fusion(bf16[2560,1792]{1,0:T(8,128)(2,1)} %convolution_convert_fusion, bf16[192,1792]{1,0:T(8,128)(2,1)S(1)} %get-tuple-element.76, bf16[192,1792]{1,0:T(8,128)(2,1)S(1)} %get-tuple-element.77, bf16[192,2560]{1,0:T(8,128)(2,1)S(1)} %copy-done.40, bf16[192,2560]{1,0:T(8,128)(2,1)S(1)} %copy-done.39), kind=kOutput, calls=%fused_computation.4 | convolution fusion | flops 3543662592 | bytes 21692416 | tf_op jit(solution)/shard_map/dot_general | solution.py:18
  593.6 13.0 %fusion.1 = bf16[1,2560,1792]{2,1,0:T(8,128)(2,1)} fusion(bf16[2560,1792]{1,0:T(8,128)(2,1)} %add_convert_fusion.5, bf16[96,1792]{1,0:T(8,128)(2,1)} %get-tuple-element.122, bf16[96,1792]{1,0:T(8,128)(2,1)} %get-tuple-element.121, bf16[192,1792]{1,0:T(8,128)(2,1)} %get-tuple-element.72, bf16[192,1792]{1,0:T(8,128)(2,1)} %get-tuple-element.73, ...), kind=kOutput, calls=%fused_computation.10 | convolution fusion | flops 5318639616 | bytes 23363584 | tf_op jit(solution)/shard_map/dot_general | solution.py:18
  606.6 12.7 %fusion = bf16[1,1792,2560]{2,1,0:T(8,128)(2,1)} fusion(bf16[1792,2560]{1,0:T(8,128)(2,1)} %add_convert_fusion.3, bf16[96,2560]{1,0:T(8,128)(2,1)} %get-tuple-element.87, bf16[96,2560]{1,0:T(8,128)(2,1)} %get-tuple-element.84, bf16[192,2560]{1,0:T(8,128)(2,1)S(1)} %copy-done.34, bf16[192,2560]{1,0:T(8,128)(2,1)S(1)} %copy-done.33, ...), kind=kOutput, calls=%fused_computation.9 | convolution fusion | flops 5318639616 | bytes 23363584 | tf_op jit(solution)/shard_map/dot_general | solution.py:18
  619.3 12.3 %fusion.2 = bf16[1,2560,1792]{2,1,0:T(8,128)(2,1)} fusion(bf16[2560,1792]{1,0:T(8,128)(2,1)} %add_convert_fusion.4, bf16[96,1792]{1,0:T(8,128)(2,1)} %get-tuple-element.120, bf16[96,1792]{1,0:T(8,128)(2,1)S(1)} %copy-done.51, bf16[192,1792]{1,0:T(8,128)(2,1)S(1)} %get-tuple-element.70, bf16[192,1792]{1,0:T(8,128)(2,1)S(1)} %get-tuple-element.71, ...), kind=kOutput, calls=%fused_computation.11 | convolution fusion | flops 5318639616 | bytes 23363584 | tf_op jit(solution)/shard_map/dot_general | solution.py:18
  (255 shorter events, 132.9 us)
Async XLA Ops:
  0.6 26.0 %collective-permute-start.5 = (bf16[192,2560]{1,0:T(8,128)(2,1)}, bf16[192,2560]{1,0:T(8,128)(2,1)}, u32[]{:S(2)}, u32[]{:S(2)}) collective-permute-start(bf16[192,2560]{1,0:T(8,128)(2,1)} %bitcast.453), channel_id=1, source_target_pairs={{0,2},{2,0},{4,6},{6,4},{8,10},{10,8},{12,14},{14,12},{1,3},{3,1},... | collective-permute-start | bytes 2949128 | tf_op jit(solution)/shard_map/ppermute | solution.py:142
  3.7 51.8 %collective-permute-start.16 = (bf16[192,2560]{1,0:T(8,128)(2,1)}, bf16[192,2560]{1,0:T(8,128)(2,1)}, u32[]{:S(2)}, u32[]{:S(2)}) collective-permute-start(bf16[192,2560]{1,0:T(8,128)(2,1)} %bitcast.454), channel_id=1, source_target_pairs={{0,1},{1,0},{2,3},{3,2},{4,5},{5,4},{6,7},{7,6},{8,9},{9,8},{10,11... | collective-permute-start | bytes 2949128 | tf_op jit(solution)/shard_map/ppermute | solution.py:146
  3.7 43.1 %collective-permute-start.6 = (bf16[192,2560]{1,0:T(8,128)(2,1)}, bf16[192,2560]{1,0:T(8,128)(2,1)}, u32[]{:S(2)}, u32[]{:S(2)}) collective-permute-start(bf16[192,2560]{1,0:T(8,128)(2,1)} %bitcast.457), channel_id=1, source_target_pairs={{0,2},{2,0},{4,6},{6,4},{8,10},{10,8},{12,14},{14,12},{1,3},{3,1},... | collective-permute-start | bytes 2949128 | tf_op jit(solution)/shard_map/ppermute | solution.py:142
  3.9 54.3 %collective-permute-start.24 = (bf16[192,2560]{1,0:T(8,128)(2,1)}, bf16[192,2560]{1,0:T(8,128)(2,1)}, u32[]{:S(2)}, u32[]{:S(2)}) collective-permute-start(bf16[192,2560]{1,0:T(8,128)(2,1)} %bitcast.458), channel_id=1, source_target_pairs={{0,1},{1,0},{2,3},{3,2},{4,5},{5,4},{6,7},{7,6},{8,9},{9,8},{10,11... | collective-permute-start | bytes 2949128 | tf_op jit(solution)/shard_map/ppermute | solution.py:146
  16.3 44.6 %collective-permute-start.1 = (bf16[192,2560]{1,0:T(8,128)(2,1)S(1)}, bf16[192,2560]{1,0:T(8,128)(2,1)}, u32[]{:S(2)}, u32[]{:S(2)}) collective-permute-start(bf16[192,2560]{1,0:T(8,128)(2,1)S(1)} %bitcast.455), channel_id=1, source_target_pairs={{0,4},{2,6},{4,0},{6,2},{8,12},{10,14},{12,8},{14,10},{1,5},{3,7},... | collective-permute-start | bytes 2949128 | tf_op jit(solution)/shard_map/ppermute | solution.py:142
  26.6 49.0 %collective-permute-start.2 = (bf16[192,2560]{1,0:T(8,128)(2,1)S(1)}, bf16[192,2560]{1,0:T(8,128)(2,1)}, u32[]{:S(2)}, u32[]{:S(2)}) collective-permute-start(bf16[192,2560]{1,0:T(8,128)(2,1)S(1)} %bitcast.459), channel_id=1, source_target_pairs={{0,4},{2,6},{4,0},{6,2},{8,12},{10,14},{12,8},{14,10},{1,5},{3,7},... | collective-permute-start | bytes 2949128 | tf_op jit(solution)/shard_map/ppermute | solution.py:142
  46.8 93.2 %collective-permute-start = (bf16[3,96,1792]{2,1,0:T(8,128)(2,1)}, bf16[3,96,1792]{2,1,0:T(8,128)(2,1)S(1)}, u32[]{:S(2)}, u32[]{:S(2)}) collective-permute-start(bf16[3,96,1792]{2,1,0:T(8,128)(2,1)} %pad_maximum_fusion.13), channel_id=1, source_target_pairs={{0,8},{2,10},{4,12},{6,14},{8,0},{10,2},{12,4},{14,6},{1,9},{3,11}... | collective-permute-start | bytes 3096584 | tf_op jit(solution)/shard_map/ppermute | solution.py:142
  55.5 392.3 %collective-permute-start.8 = (bf16[3,192,1792]{2,1,0:T(8,128)(2,1)}, bf16[3,192,1792]{2,1,0:T(8,128)(2,1)}, u32[]{:S(2)}, u32[]{:S(2)}) collective-permute-start(bf16[3,192,1792]{2,1,0:T(8,128)(2,1)} %pad_maximum_fusion.2), channel_id=1, source_target_pairs={{0,8},{2,10},{4,12},{6,14},{8,0},{10,2},{12,4},{14,6},{1,9},{3,11}... | collective-permute-start | bytes 6193160 | tf_op jit(solution)/shard_map/ppermute | solution.py:142
  58.2 140.0 %collective-permute-start.21 = (bf16[192,2560]{1,0:T(8,128)(2,1)}, bf16[192,2560]{1,0:T(8,128)(2,1)}, u32[]{:S(2)}, u32[]{:S(2)}) collective-permute-start(bf16[192,2560]{1,0:T(8,128)(2,1)} %collective-permute-done.5), channel_id=1, source_target_pairs={{0,1},{1,0},{2,3},{3,2},{4,5},{5,4},{6,7},{7,6},{8,9},{9,8},{10,11... | collective-permute-start | bytes 2949128 | tf_op jit(solution)/shard_map/ppermute | solution.py:146
  60.8 140.3 %collective-permute-start.25 = (bf16[192,2560]{1,0:T(8,128)(2,1)}, bf16[192,2560]{1,0:T(8,128)(2,1)}, u32[]{:S(2)}, u32[]{:S(2)}) collective-permute-start(bf16[192,2560]{1,0:T(8,128)(2,1)} %collective-permute-done.6), channel_id=1, source_target_pairs={{0,1},{1,0},{2,3},{3,2},{4,5},{5,4},{6,7},{7,6},{8,9},{9,8},{10,11... | collective-permute-start | bytes 2949128 | tf_op jit(solution)/shard_map/ppermute | solution.py:146
  75.6 77.5 %collective-permute-start.3 = (bf16[192,2560]{1,0:T(8,128)(2,1)}, bf16[192,2560]{1,0:T(8,128)(2,1)}, u32[]{:S(2)}, u32[]{:S(2)}) collective-permute-start(bf16[192,2560]{1,0:T(8,128)(2,1)} %collective-permute-done.1), channel_id=1, source_target_pairs={{0,2},{2,0},{4,6},{6,4},{8,10},{10,8},{12,14},{14,12},{1,3},{3,1},... | collective-permute-start | bytes 2949128 | tf_op jit(solution)/shard_map/ppermute | solution.py:142
  140.0 20.7 %collective-permute-start.4 = (bf16[192,2560]{1,0:T(8,128)(2,1)}, bf16[192,2560]{1,0:T(8,128)(2,1)S(1)}, u32[]{:S(2)}, u32[]{:S(2)}) collective-permute-start(bf16[192,2560]{1,0:T(8,128)(2,1)} %collective-permute-done.2), channel_id=1, source_target_pairs={{0,2},{2,0},{4,6},{6,4},{8,10},{10,8},{12,14},{14,12},{1,3},{3,1},... | collective-permute-start | bytes 2949128 | tf_op jit(solution)/shard_map/ppermute | solution.py:142
  153.1 51.0 %collective-permute-start.15 = (bf16[192,2560]{1,0:T(8,128)(2,1)}, bf16[192,2560]{1,0:T(8,128)(2,1)}, u32[]{:S(2)}, u32[]{:S(2)}) collective-permute-start(bf16[192,2560]{1,0:T(8,128)(2,1)} %collective-permute-done.1), channel_id=1, source_target_pairs={{0,1},{1,0},{2,3},{3,2},{4,5},{5,4},{6,7},{7,6},{8,9},{9,8},{10,11... | collective-permute-start | bytes 2949128 | tf_op jit(solution)/shard_map/ppermute | solution.py:146
  160.6 49.4 %collective-permute-start.29 = (bf16[192,2560]{1,0:T(8,128)(2,1)}, bf16[192,2560]{1,0:T(8,128)(2,1)}, u32[]{:S(2)}, u32[]{:S(2)}) collective-permute-start(bf16[192,2560]{1,0:T(8,128)(2,1)} %collective-permute-done.2), channel_id=1, source_target_pairs={{0,1},{1,0},{2,3},{3,2},{4,5},{5,4},{6,7},{7,6},{8,9},{9,8},{10,11... | collective-permute-start | bytes 2949128 | tf_op jit(solution)/shard_map/ppermute | solution.py:146
  164.7 31.9 %copy-start.22 = (bf16[192,1792]{1,0:T(8,128)(2,1)}, bf16[192,1792]{1,0:T(8,128)(2,1)S(1)}, u32[]{:S(2)}) copy-start(bf16[192,1792]{1,0:T(8,128)(2,1)S(1)} %fusion.135) | copy-start | bytes 2064388
  198.2 17.7 %collective-permute-start.22 = (bf16[3,96,1792]{2,1,0:T(8,128)(2,1)S(1)}, bf16[3,96,1792]{2,1,0:T(8,128)(2,1)S(1)}, u32[]{:S(2)}, u32[]{:S(2)}) collective-permute-start(bf16[3,96,1792]{2,1,0:T(8,128)(2,1)S(1)} %copy-done.30), channel_id=1, source_target_pairs={{0,1},{1,0},{2,3},{3,2},{4,5},{5,4},{6,7},{7,6},{8,9},{9,8},{10,11... | collective-permute-start | bytes 3096584 | tf_op jit(solution)/shard_map/ppermute | solution.py:146
  201.1 290.1 %collective-permute-start.10 = (bf16[3,192,1792]{2,1,0:T(8,128)(2,1)}, bf16[3,192,1792]{2,1,0:T(8,128)(2,1)}, u32[]{:S(2)}, u32[]{:S(2)}) collective-permute-start(bf16[3,192,1792]{2,1,0:T(8,128)(2,1)} %pad_maximum_fusion.3), channel_id=1, source_target_pairs={{0,8},{2,10},{4,12},{6,14},{8,0},{10,2},{12,4},{14,6},{1,9},{3,11}... | collective-permute-start | bytes 6193160 | tf_op jit(solution)/shard_map/ppermute | solution.py:142
  204.1 265.8 %collective-permute-start.11 = (bf16[3,192,1792]{2,1,0:T(8,128)(2,1)}, bf16[3,192,1792]{2,1,0:T(8,128)(2,1)}, u32[]{:S(2)}, u32[]{:S(2)}) collective-permute-start(bf16[3,192,1792]{2,1,0:T(8,128)(2,1)} %pad_maximum_fusion.4), channel_id=1, source_target_pairs={{0,8},{2,10},{4,12},{6,14},{8,0},{10,2},{12,4},{14,6},{1,9},{3,11}... | collective-permute-start | bytes 6193160 | tf_op jit(solution)/shard_map/ppermute | solution.py:142
  210.0 209.6 %collective-permute-start.7 = (bf16[2,96,1792]{2,1,0:T(8,128)(2,1)S(1)}, bf16[2,96,1792]{2,1,0:T(8,128)(2,1)S(1)}, u32[]{:S(2)}, u32[]{:S(2)}) collective-permute-start(bf16[2,96,1792]{2,1,0:T(8,128)(2,1)S(1)} %pad_maximum_fusion.15), channel_id=1, source_target_pairs={{0,8},{2,10},{4,12},{6,14},{8,0},{10,2},{12,4},{14,6},{1,9},{3,11}... | collective-permute-start | bytes 2064392 | tf_op jit(solution)/shard_map/ppermute | solution.py:142
  215.9 210.6 %copy-start.45 = (bf16[192,2560]{1,0:T(8,128)(2,1)S(1)}, bf16[192,2560]{1,0:T(8,128)(2,1)}, u32[]{:S(2)}) copy-start(bf16[192,2560]{1,0:T(8,128)(2,1)} %copy-done.43) | copy-start | bytes 2949124
  215.9 210.6 %collective-permute-start.14 = (bf16[1,96,1792]{2,1,0:T(8,128)(2,1)S(1)}, bf16[1,96,1792]{2,1,0:T(8,128)(2,1)S(1)}, u32[]{:S(2)}, u32[]{:S(2)}) collective-permute-start(bf16[1,96,1792]{2,1,0:T(8,128)(2,1)S(1)} %bitcast.486), channel_id=1, source_target_pairs={{0,8},{2,10},{4,12},{6,14},{8,0},{10,2},{12,4},{14,6},{1,9},{3,11}... | collective-permute-start | bytes 1032200 | tf_op jit(solution)/shard_map/ppermute | solution.py:142
  419.6 20.3 %collective-permute-start.19 = (bf16[192,2560]{1,0:T(8,128)(2,1)}, bf16[192,2560]{1,0:T(8,128)(2,1)S(1)}, u32[]{:S(2)}, u32[]{:S(2)}) collective-permute-start(bf16[192,2560]{1,0:T(8,128)(2,1)} %collective-permute-done.3), channel_id=1, source_target_pairs={{0,1},{1,0},{2,3},{3,2},{4,5},{5,4},{6,7},{7,6},{8,9},{9,8},{10,11... | collective-permute-start | bytes 2949128 | tf_op jit(solution)/shard_map/ppermute | solution.py:146
  426.5 16.6 %collective-permute-start.26 = (bf16[192,2560]{1,0:T(8,128)(2,1)S(1)}, bf16[192,2560]{1,0:T(8,128)(2,1)S(1)}, u32[]{:S(2)}, u32[]{:S(2)}) collective-permute-start(bf16[192,2560]{1,0:T(8,128)(2,1)S(1)} %copy-done.45), channel_id=1, source_target_pairs={{0,1},{1,0},{2,3},{3,2},{4,5},{5,4},{6,7},{7,6},{8,9},{9,8},{10,11... | collective-permute-start | bytes 2949128 | tf_op jit(solution)/shard_map/ppermute | solution.py:146
  439.9 4.6 collective-permute-start.18
  443.1 2.9 collective-permute-start.27
  444.5 2.4 collective-permute-start.28
  467.2 164.5 %collective-permute-start.9 = (bf16[2,192,2560]{2,1,0:T(8,128)(2,1)}, bf16[2,192,2560]{2,1,0:T(8,128)(2,1)}, u32[]{:S(2)}, u32[]{:S(2)}) collective-permute-start(bf16[2,192,2560]{2,1,0:T(8,128)(2,1)} %pad_maximum_fusion.8), channel_id=1, source_target_pairs={{0,2},{2,0},{4,6},{6,4},{8,10},{10,8},{12,14},{14,12},{1,3},{3,1},... | collective-permute-start | bytes 5898248 | tf_op jit(solution)/shard_map/ppermute | solution.py:142
  469.9 42.1 %collective-permute-start.23 = (bf16[3,192,1792]{2,1,0:T(8,128)(2,1)}, bf16[3,192,1792]{2,1,0:T(8,128)(2,1)}, u32[]{:S(2)}, u32[]{:S(2)}) collective-permute-start(bf16[3,192,1792]{2,1,0:T(8,128)(2,1)} %pad_maximum_fusion.7), channel_id=1, source_target_pairs={{0,1},{1,0},{2,3},{3,2},{4,5},{5,4},{6,7},{7,6},{8,9},{9,8},{10,11... | collective-permute-start | bytes 6193160 | tf_op jit(solution)/shard_map/ppermute | solution.py:146
  488.6 65.8 %collective-permute-start.12 = (bf16[2,192,2560]{2,1,0:T(8,128)(2,1)}, bf16[2,192,2560]{2,1,0:T(8,128)(2,1)}, u32[]{:S(2)}, u32[]{:S(2)}) collective-permute-start(bf16[2,192,2560]{2,1,0:T(8,128)(2,1)} %pad_maximum_fusion.9), channel_id=1, source_target_pairs={{0,2},{2,0},{4,6},{6,4},{8,10},{10,8},{12,14},{14,12},{1,3},{3,1},... | collective-permute-start | bytes 5898248 | tf_op jit(solution)/shard_map/ppermute | solution.py:142
  491.0 65.7 %collective-permute-start.20 = (bf16[3,192,1792]{2,1,0:T(8,128)(2,1)}, bf16[3,192,1792]{2,1,0:T(8,128)(2,1)}, u32[]{:S(2)}, u32[]{:S(2)}) collective-permute-start(bf16[3,192,1792]{2,1,0:T(8,128)(2,1)} %pad_maximum_fusion.6), channel_id=1, source_target_pairs={{0,1},{1,0},{2,3},{3,2},{4,5},{5,4},{6,7},{7,6},{8,9},{9,8},{10,11... | collective-permute-start | bytes 6193160 | tf_op jit(solution)/shard_map/ppermute | solution.py:146
  495.5 95.0 %collective-permute-start.17 = (bf16[3,192,1792]{2,1,0:T(8,128)(2,1)}, bf16[3,192,1792]{2,1,0:T(8,128)(2,1)}, u32[]{:S(2)}, u32[]{:S(2)}) collective-permute-start(bf16[3,192,1792]{2,1,0:T(8,128)(2,1)} %pad_maximum_fusion.5), channel_id=1, source_target_pairs={{0,1},{1,0},{2,3},{3,2},{4,5},{5,4},{6,7},{7,6},{8,9},{9,8},{10,11... | collective-permute-start | bytes 6193160 | tf_op jit(solution)/shard_map/ppermute | solution.py:146
  556.6 75.1 %collective-permute-start.13 = (bf16[2,192,2560]{2,1,0:T(8,128)(2,1)S(1)}, bf16[2,192,2560]{2,1,0:T(8,128)(2,1)S(1)}, u32[]{:S(2)}, u32[]{:S(2)}) collective-permute-start(bf16[2,192,2560]{2,1,0:T(8,128)(2,1)S(1)} %fusion.63), channel_id=1, source_target_pairs={{0,4},{2,6},{4,0},{6,2},{8,12},{10,14},{12,8},{14,10},{1,5},{3,7},... | collective-permute-start | bytes 5898248 | tf_op jit(solution)/shard_map/ppermute | solution.py:142
  (71 other events, 542.5 us)
